TPU v7x, 32 devices: a whole 2x2x4 slice. The times are simulated.
32 devices in a mesh: gx: 4 (over y, x), gy: 8 (over z, core).
Axes of the slice: x: 2, y: 2, z: 4, core: 2. Of those that a mesh axis runs over, the one named last changes fastest.
Arguments:
- node_shift: float32 [2, 256, 4096], P(None, 'gx', 'gy'), may hold values from -1.5 to 1.5
- node_speed: float32 [2, 256, 4096], P(None, 'gx', 'gy'), may hold values from -4 to 4
- damage_initial: int32 [2, 256, 4096], P(None, 'gx', 'gy'), may hold values from 0 to 7
- cohesive_markers: int32 [32, 8], P('gx', 'gy'), may hold values from 0 to 1, as said below
- cell_warmth: float32 [128, 2048], P(('gx', 'gy')), may hold values from 0 to 1
- heat_storage: float32 [128, 2048], P(('gx', 'gy')), may hold values from 0.5 to 2
- surface_transfer: float32 [128, 2048], P(('gx', 'gy')), may hold values from 0.1 to 1
- quench_liquid_heat: float32 [128, 2048], P(('gx', 'gy')), may hold values from 0 to 0.3
Outputs:
- displace_new: float32 [2, 256, 4096], P(None, 'gx', 'gy')
- velocity_new: float32 [2, 256, 4096], P(None, 'gx', 'gy')
- damage: bfloat16 [2, 256, 4096], P(None, 'gx', 'gy')
- warmth_after_solve: float32 [128, 2048], P(('gx', 'gy'))
Inputs may be any that keep to these rules, and one draw needn't show every extreme that they name: `cohesive_markers`: within each column, every block of 8 consecutive tile rows starting at a multiple of 8 holds between 1 and 4 ones, and in every draw some block holds exactly 4.
All inputs are finite; a program needn't handle non-finite values.
Results may differ from a plain program's by a relative error of at most 0.001.
Values sent between devices are 32-bit elements; how exact they have to be, the bound alone decides.
A program may use at most 64 MiB of HBM per device.

v0:
```python
import functools

import jax
import jax.numpy as jnp
from jax import lax
from jax.experimental import pallas as pl
from jax.experimental.pallas import tpu as pltpu
from jax.sharding import PartitionSpec as P

SR = 8
SEG = 128
SUBSTEPS = 8
HALO = 8
MESH = pl.DeviceIdType.MESH
F32 = jnp.float32


def lane_iota(shape):
    return lax.broadcasted_iota(jnp.int32, shape, 1)


def row_iota(shape):
    return lax.broadcasted_iota(jnp.int32, shape, 0)


def full_dot(a, b):
    return jnp.dot(a, b, precision=lax.Precision.HIGHEST, preferred_element_type=F32)


def kernel(
    n_gx,
    n_gy,
    shift,
    speed,
    level_h,
    mark,
    warm_h,
    store_h,
    film_h,
    bath_h,
    o_shift,
    o_speed,
    o_dam,
    o_warm,
    tsend,
    trecv,
    asend,
    arecv,
    pk_l,
    pk_r,
    rk_l,
    rk_r,
    wsend,
    wrecv,
    rowsend,
    rowrecv,
    keep,
    hist,
    level,
    warm,
    store,
    film,
    bath,
    state,
    wt,
    tx,
    ty,
    tc,
    acf,
    widebuf,
    gap,
    cbuf,
    crow,
    ccl,
    ccr,
    zsend,
    zrecv,
    msend,
    mrecv,
    nb_send,
    nb_recv,
    t_sem,
    a_sem,
    c_send,
    c_recv,
    z_sem,
    m_sem,
    in_sem,
    dambuf,
    warmbuf,
    out_sem,
):
    ndev = n_gx * n_gy
    gx = lax.axis_index("gx")
    gy = lax.axis_index("gy")
    me = gx * n_gy + gy
    _, hh, ww = shift.shape
    rpd, _ = warm_h.shape
    cw = ww // 2
    ch = hh // 2
    hb = HALO // rpd
    nsl = n_gy + 2 * hb
    up = lax.rem(gx + n_gx - 1, n_gx)
    down = lax.rem(gx + 1, n_gx)
    left = lax.rem(gy + n_gy - 1, n_gy)
    right = lax.rem(gy + 1, n_gy)

    own_r = slice(HALO, HALO + hh)
    loads = [
        pltpu.make_async_copy(src, dst, in_sem.at[i])
        for i, (src, dst) in enumerate(
            (
                (warm_h, warm),
                (level_h, level),
                (shift, state.at[0:2, own_r, 0:ww]),
                (speed, state.at[2:4, own_r, 0:ww]),
                (store_h, store),
                (film_h, film),
                (bath_h, bath),
            )
        )
    ]
    for copy in loads:
        copy.start()
    barrier = pltpu.get_barrier_semaphore()

    def greet(k, c):
        t = lax.rem(me + k, ndev)
        pl.semaphore_signal(barrier, inc=1, device_id=(t // n_gy, t % n_gy), device_id_type=MESH)
        return c

    lax.fori_loop(1, ndev, greet, 0)

    lane = lane_iota((hh, 128))
    for s in range(hh // SR):
        wt[HALO + SR * s : HALO + SR * s + SR, 0:ww] = jnp.full((SR, ww), mark[0, s], jnp.int32).astype(F32)
    w_own = wt[own_r, 0:ww]
    grow = gx * hh + row_iota((hh, ww))
    gcol = gy * ww + lane_iota((hh, ww))
    loads[1].wait()
    state[4, own_r, 0:ww] = jnp.where(grow >= 1, level[0].astype(F32) * 0.125 * w_own, 1.0)
    state[5, own_r, 0:ww] = jnp.where(gcol >= 1, level[1].astype(F32) * 0.125 * w_own, 1.0)
    wsend[0] = wt[HALO : HALO + 8, 0:128]
    wsend[1] = wt[HALO + hh - 8 : HALO + hh, 0:128]
    loads[2].wait()
    loads[3].wait()
    acc_l = jnp.zeros((hh, 128), F32)
    acc_r = jnp.zeros((hh, 128), F32)
    for f in range(7):
        field = state.at[f] if f < 6 else wt
        first, last = field[own_r, 0:128], field[own_r, ww - 128 : ww]
        here = (lane >= 8 * f) & (lane < 8 * f + 8)
        first = pltpu.roll(first, 8 * f, 1) if f else first
        acc_l = jnp.where(here, first, acc_l)
        acc_r = jnp.where(here, pltpu.roll(last, 8 * f + 8, 1), acc_r)
        if f < 6:
            rowsend[0, f] = field[HALO : HALO + 8, 0:ww]
            rowsend[1, f] = field[HALO + hh - 8 : HALO + hh, 0:ww]
    pk_l[...] = acc_l
    pk_r[...] = acc_r

    lane_c = lane_iota((rpd, 128))

    def chunk(value, k):
        after = value[:, (cw * (k + 1)) % (cw * n_gy) :][:, 0:128]
        before = value[:, (cw * k - 128) % (cw * n_gy) :][:, 0:128]
        return value[:, cw * k : cw * k + cw], jnp.where(lane_c < 64, after, before)

    for i in (0, 4, 5, 6):
        loads[i].wait()
    t_own = warm[...]
    base = store[...] + film[...]
    force_own = store[...] * t_own + film[...] * bath[...]
    for k in range(n_gy):
        main, edge = chunk(t_own, k)
        tsend[k, :, 0:cw] = main
        tsend[k, :, cw : cw + 128] = edge
        for q, val in enumerate((base, force_own)):
            main, edge = chunk(val, k)
            asend[k, q, :, 0:cw] = main
            asend[k, q, :, cw : cw + 128] = edge

    pl.semaphore_wait(barrier, ndev - 1)

    def remote(src, dst, ssem, rsem, where):
        return pltpu.make_async_remote_copy(
            src_ref=src, dst_ref=dst, send_sem=ssem, recv_sem=rsem, device_id=where,
            device_id_type=MESH,
        )

    def neighbours(send_l, send_r, row_u, row_d, recv_l, recv_r, got_u, got_d, rows, ssem, rsem):
        top, end = slice(0, 8), slice(rows - 8, rows)
        lo, mid, hi = slice(0, 8), slice(8, rows + 8), slice(rows + 8, rows + 16)
        return [
            remote(row_u, got_d, ssem.at[0], rsem.at[0], (up, gy)),
            remote(row_d, got_u, ssem.at[1], rsem.at[1], (down, gy)),
            remote(send_l, recv_r.at[mid], ssem.at[2], rsem.at[2], (gx, left)),
            remote(send_r, recv_l.at[mid], ssem.at[3], rsem.at[3], (gx, right)),
            remote(send_l.at[top], recv_r.at[hi], ssem.at[4], rsem.at[4], (up, left)),
            remote(send_r.at[top], recv_l.at[hi], ssem.at[5], rsem.at[5], (up, right)),
            remote(send_l.at[end], recv_r.at[lo], ssem.at[6], rsem.at[6], (down, left)),
            remote(send_r.at[end], recv_l.at[lo], ssem.at[7], rsem.at[7], (down, right)),
        ]

    first = neighbours(
        pk_l,
        pk_r,
        rowsend.at[0],
        rowsend.at[1],
        rk_l,
        rk_r,
        rowrecv.at[0],
        rowrecv.at[1],
        hh,
        nb_send,
        nb_recv,
    ) + [
        remote(wsend.at[0], wrecv.at[1], nb_send.at[8], nb_recv.at[8], (up, gy)),
        remote(wsend.at[1], wrecv.at[0], nb_send.at[9], nb_recv.at[9], (down, gy)),
    ]

    def spread_out(send, recv, sem):
        def along(k, c):
            t = lax.rem(gy + k, n_gy)
            remote(send.at[t], recv.at[gy + hb], sem.at[1], sem.at[0], (gx, t)).start()
            return c

        lax.fori_loop(1, n_gy, along, 0)
        pltpu.make_async_copy(send.at[gy], recv.at[gy + hb], sem.at[0]).start()

        @pl.when(gy < hb)
        def _():
            def go(k, c):
                remote(
                    send.at[k], recv.at[gy + hb + n_gy], sem.at[2], sem.at[0], (up, k)
                ).start()
                return c

            lax.fori_loop(0, n_gy, go, 0)

        @pl.when(gy >= n_gy - hb)
        def _():
            def go(k, c):
                remote(
                    send.at[k], recv.at[gy - (n_gy - hb)], sem.at[3], sem.at[0], (down, k)
                ).start()
                return c

            lax.fori_loop(0, n_gy, go, 0)

    def spread_sent(send, recv, sem):
        part = pl.ds(0, n_gy - 1)
        remote(send.at[part], recv.at[part], sem.at[1], sem.at[0], (gx, right)).wait_send()
        whole = pl.ds(0, n_gy)

        @pl.when(gy < hb)
        def _():
            remote(send, recv.at[whole], sem.at[2], sem.at[0], (up, gy)).wait_send()

        @pl.when(gy >= n_gy - hb)
        def _():
            remote(send, recv.at[whole], sem.at[3], sem.at[0], (down, gy)).wait_send()

    spread_out(tsend, trecv, t_sem)
    for copy in first:
        copy.start()

    pltpu.make_async_copy(trecv, trecv, t_sem.at[0]).wait()

    def late(k, c):
        t = lax.rem(gy + k, n_gy)
        remote(asend.at[t], arecv.at[gy], a_sem.at[1], a_sem.at[0], (gx, t)).start()
        return c

    lax.fori_loop(1, n_gy, late, 0)
    pltpu.make_async_copy(asend.at[gy], arecv.at[gy], a_sem.at[0]).start()
    crows = ch + 16
    for k in range(nsl):
        tc[rpd * k : rpd * k + rpd, :] = trecv[k]
    cshape = (crows, cw + 128)
    crow_i, clane_i = row_iota(cshape), lane_iota(cshape)
    t_all = tc[...]
    p = t_all
    p = jnp.where((gx == 0) & (crow_i < 8), t_all[8:9, :], p)
    p = jnp.where((gx == n_gx - 1) & (crow_i >= ch + 8), t_all[ch + 7 : ch + 8, :], p)
    wide = cw + 128
    q = jnp.where((gy == 0) & (clane_i == wide - 1), pltpu.roll(p, wide - 1, 1), p)
    q = jnp.where((gy == n_gy - 1) & (clane_i == cw), pltpu.roll(p, 1, 1), q)
    even = 0.75 * q + 0.25 * pltpu.roll(q, 1, 0)
    odd = 0.75 * q + 0.25 * pltpu.roll(q, crows - 1, 0)
    frows = hh + 2 * HALO
    need = frows // 2
    ntile = wide // 128
    for t in range(ntile):
        cols = slice(128 * t, 128 * t + 128)
        widebuf[t, pl.ds(0, need, stride=2), :] = even[4 : 4 + need, cols]
        widebuf[t, pl.ds(1, need, stride=2), :] = odd[4 : 4 + need, cols]
    r = jnp.concatenate([widebuf[t] for t in range(ntile)], axis=1)
    ecol = 0.75 * r + 0.25 * pltpu.roll(r, 1, 1)
    ocol = 0.75 * r + 0.25 * pltpu.roll(r, wide - 1, 1)
    k_i, n_i = row_iota((256, 256)), lane_iota((256, 256))
    weave = (n_i == jnp.where(k_i < 128, 2 * k_i, 2 * k_i - 255)).astype(F32)
    stack = jnp.concatenate(
        [
            jnp.concatenate([ecol[:, 128 * t : 128 * t + 128], ocol[:, 128 * t : 128 * t + 128]], 1)
            for t in range(ntile)
        ],
        axis=0,
    )
    woven = full_dot(stack, weave)
    lane_f = lane_iota((frows, 128))
    pieces = [woven[frows * t : frows * t + frows] for t in range(ntile)]
    edge = jnp.where(lane_f < 64, pieces[-1][:, 0:128], pieces[-1][:, 128:256])
    fine = jnp.concatenate(pieces[:-1] + [edge], axis=1)
    fwide = ww + 128
    tx[...] = 0.6 * (0.5 * (fine + pltpu.roll(fine, 1, 0)))
    ty[...] = 0.6 * (0.5 * (fine + pltpu.roll(fine, 1, 1)))

    for copy in first[2:8]:
        copy.wait_recv()
    got_l, got_r = rk_l[...], rk_r[...]
    for f in range(7):
        from_r = pltpu.roll(got_r, 128 - 8 * f, 1) if f else got_r
        from_l = pltpu.roll(got_l, 120 - 8 * f, 1)
        side = jnp.where(lane_f < 8, from_r, jnp.where(lane_f >= 120, from_l, 0.0))
        if f == 5:
            off_l = (gy == 0) & (lane_f >= 64)
            off_r = (gy == n_gy - 1) & (lane_f < 64)
            side = jnp.where(off_l | off_r, 1.0, side)
        target = state.at[f] if f < 6 else wt
        target[:, ww:fwide] = side
    sub = row_iota((8, fwide))
    last_strip = frows // 8 - 1

    def edges(s, old):
        rows = slice(8 * s, 8 * s + 8)
        u0, u1 = state[0, rows, :], state[1, rows, :]
        w = wt[rows, :]
        r0, r1 = pltpu.roll(u0, 1, 0), pltpu.roll(u1, 1, 0)
        p0 = jnp.where(sub == 0, old["r0"], r0) if old else r0
        p1 = jnp.where(sub == 0, old["r1"], r1) if old else r1
        open_x = u0 - p0 - tx[rows, :]
        st = jnp.maximum(open_x, 0.0)
        dx = jnp.maximum(state[4, rows, :], (1.0 - jnp.exp(st * st * -4.0)) * w)
        state[4, rows, :] = dx
        sp = 1.0 - dx
        nx = sp * open_x
        ax = sp * (u1 - p1)
        open_y = u1 - pltpu.roll(u1, 1, 1) - ty[rows, :]
        st = jnp.maximum(open_y, 0.0)
        dy = jnp.maximum(state[5, rows, :], (1.0 - jnp.exp(st * st * -4.0)) * w)
        state[5, rows, :] = dy
        sp = 1.0 - dy
        ny = sp * open_y
        ay = sp * (u0 - pltpu.roll(u0, 1, 1))
        return dict(
            r0=r0, r1=r1, nx=nx, ax=ax, u0=u0, u1=u1,
            sx=pltpu.roll(nx, 7, 0), sa=pltpu.roll(ax, 7, 0),
            fy0=pltpu.roll(ay, fwide - 1, 1) - ay,
            fy1=pltpu.roll(ny, fwide - 1, 1) - ny,
        )

    def advance(s, old, new):
        rows = slice(8 * s, 8 * s + 8)
        nn = jnp.where(sub == 7, new["sx"], old["sx"])
        na = jnp.where(sub == 7, new["sa"], old["sa"])
        f0 = (nn - old["nx"]) + old["fy0"]
        f1 = (na - old["ax"]) + old["fy1"]
        v0, v1 = state[2, rows, :], state[3, rows, :]
        v0 = v0 + 0.4 * (f0 - 0.05 * v0)
        v1 = v1 + 0.4 * (f1 - 0.05 * v1)
        state[2, rows, :] = v0
        state[3, rows, :] = v1
        state[0, rows, :] = old["u0"] + 0.4 * v0
        state[1, rows, :] = old["u1"] + 0.4 * v1

    redo = (slice(8, 16), slice(8 * last_strip - 8, 8 * last_strip))
    for i, rows in enumerate(redo):
        keep[i] = state[:, rows, :]

    def interior(t, c):
        old = None
        for s in range(1, last_strip):
            new = edges(s, old)
            if s == 2:
                hist[t, 0] = new["sx"]
                hist[t, 1] = new["sa"]
            if s == last_strip - 2:
                hist[t, 2] = new["r0"]
                hist[t, 3] = new["r1"]
            if old:
                advance(s - 1, old, new)
            old = new
        advance(last_strip - 1, old, old)
        return c

    lax.fori_loop(0, SUBSTEPS, interior, 0)

    pltpu.make_async_copy(arecv, arecv, a_sem.at[0]).wait()
    for k in range(n_gy):
        for q in range(2):
            acf[q, 8 + rpd * k : 8 + rpd * k + rpd, :] = arecv[k, q]
    coarse_rows = [
        remote(
            acf.at[:, 8:16], acf.at[:, ch + 8 : ch + 16], a_sem.at[2], a_sem.at[4], (up, gy)
        ),
        remote(acf.at[:, ch : ch + 8], acf.at[:, 0:8], a_sem.at[3], a_sem.at[5], (down, gy)),
    ]
    for copy in coarse_rows:
        copy.start()

    for copy in first[0:2] + first[8:10]:
        copy.wait_recv()
    for i, rows in enumerate(redo):
        state[:, rows, :] = keep[i]
    for side_row, at in ((0, 0), (1, hh + HALO)):
        state[:, at : at + 8, 0:ww] = rowrecv[side_row]
        for t in range(ww // 128):
            wt[at : at + 8, 128 * t : 128 * t + 128] = wrecv[side_row]

    @pl.when(gx == 0)
    def _():
        state[4, 0:8, :] = jnp.ones((8, fwide), F32)

    @pl.when(gx == n_gx - 1)
    def _():
        state[4, hh + HALO : hh + HALO + 8, :] = jnp.ones((8, fwide), F32)

    def border(t, c):
        e0 = edges(0, None)
        e1 = edges(1, e0)
        advance(0, e0, e1)
        advance(1, e1, dict(sx=hist[t, 0], sa=hist[t, 1]))
        e8 = edges(last_strip - 1, dict(r0=hist[t, 2], r1=hist[t, 3]))
        e9 = edges(last_strip, e8)
        advance(last_strip - 1, e8, e9)
        advance(last_strip, e9, e9)
        return c

    lax.fori_loop(0, SUBSTEPS, border, 0)

    dam_x = jnp.where(grow >= 1, state[4, own_r, 0:ww], 0.0)
    dam_y = jnp.where(gcol >= 1, state[5, own_r, 0:ww], 0.0)
    both = dam_x + dam_y
    for t in range(ww // 128):
        gap[t] = both[:, 128 * t : 128 * t + 128]
    rows2 = jnp.concatenate(
        [
            gap[t, pl.ds(0, ch, stride=2), :] + gap[t, pl.ds(1, ch, stride=2), :]
            for t in range(ww // 128)
        ],
        axis=1,
    )
    k_i, n_i = row_iota((256, 128)), lane_iota((256, 128))
    pos = (k_i % SEG).astype(F32)
    col = (2 * (n_i % 64)).astype(F32)
    tab = jnp.exp(jnp.abs(pos - col) * (-4.0 / SEG)) + jnp.exp(jnp.abs(pos - col - 1.0) * (-4.0 / SEG))
    tab = jnp.where(k_i // SEG == n_i // 64, tab * (1.0 / SEG), 0.0)
    npair = ww // 256
    glow = full_dot(
        jnp.concatenate([rows2[:, 256 * t : 256 * t + 256] for t in range(npair)], axis=0), tab
    )
    resist = jnp.concatenate([glow[ch * t : ch * t + ch] for t in range(npair)], axis=1)
    cond_own = (1.0 + 0.5 * tc[8 : 8 + ch, 0:cw]) / (1.0 + resist)
    cbuf[...] = cond_own
    second = neighbours(
        cbuf.at[:, 0:128], cbuf.at[:, cw - 128 : cw], cbuf.at[0:8], cbuf.at[ch - 8 : ch],
        ccl, ccr, crow.at[0], crow.at[1], ch, c_send, c_recv,
    )
    for copy in second:
        copy.start()

    dambuf[0] = dam_x.astype(jnp.bfloat16)
    dambuf[1] = dam_y.astype(jnp.bfloat16)
    puts = [
        pltpu.make_async_copy(src, dst, out_sem.at[i])
        for i, (src, dst) in enumerate(
            (
                (state.at[0:2, own_r, 0:ww], o_shift),
                (state.at[2:4, own_r, 0:ww], o_speed),
                (dambuf, o_dam),
                (warmbuf, o_warm),
            )
        )
    ]
    for copy in puts[0:3]:
        copy.start()

    for copy in coarse_rows:
        copy.wait_recv()

    for copy in second:
        copy.wait_recv()
    lane_k = lane_iota((crows, 128))
    cond = jnp.concatenate(
        [
            jnp.concatenate([crow[0], cbuf[...], crow[1]], axis=0),
            jnp.where(lane_k < 64, ccr[...], ccl[...]),
        ],
        axis=1,
    )
    crow_g = gx * ch - 8 + crow_i
    ccol_g = gy * cw + jnp.where(clane_i < cw + 64, clane_i, clane_i - wide)

    def four(x):
        return (
            pltpu.roll(x, 1, 0),
            pltpu.roll(x, crows - 1, 0),
            pltpu.roll(x, 1, 1),
            pltpu.roll(x, wide - 1, 1),
        )

    masks = (
        crow_g >= 1,
        crow_g <= ch * n_gx - 2,
        ccol_g >= 1,
        ccol_g <= cw * n_gy - 2,
    )
    faces = [
        jnp.where(m, 0.5 * (cond + nb), 0.0) for m, nb in zip(masks, four(cond))
    ]
    offsum = faces[0] + faces[1] + faces[2] + faces[3]
    diagonal = acf[0] + offsum
    ratio = offsum / diagonal
    peak = jnp.max(ratio[8 : 8 + ch, 0:cw])
    msend[...] = jnp.full((1, 128), peak, F32)

    def tell(k, c):
        t = lax.rem(me + k, ndev)
        remote(
            msend, mrecv.at[k - 1], m_sem.at[1], m_sem.at[0], (t // n_gy, t % n_gy)
        ).start()
        return c

    lax.fori_loop(1, ndev, tell, 0)

    t_all = tc[...]
    near = sum(f * nb for f, nb in zip(faces, four(t_all)))
    z = (acf[1] - (diagonal * t_all - near)) / diagonal
    faces = [f / diagonal for f in faces]
    for j in range(4):
        if j:
            z = z - sum(f * nb for f, nb in zip(faces, four(z)))
        for k in range(n_gy):
            zsend[k, j] = z[8 + rpd * k : 8 + rpd * k + rpd, 0:cw]

    def home(k, c):
        t = lax.rem(gy + k, n_gy)
        remote(zsend.at[t], zrecv.at[gy], z_sem.at[1], z_sem.at[0], (gx, t)).start()
        return c

    lax.fori_loop(1, n_gy, home, 0)
    pltpu.make_async_copy(zsend.at[gy], zrecv.at[gy], z_sem.at[0]).start()

    pltpu.make_async_copy(mrecv, mrecv, m_sem.at[0]).wait()
    peak = jnp.maximum(jnp.max(mrecv[...], axis=0), msend[...])[0:1, :]
    low, high = 1.0 - peak, 1.0 + peak
    center = 0.5 * (high + low)
    spread = 0.5 * (high - low)
    sigma = center / spread
    rho = 1.0 / sigma
    zero = jnp.zeros_like(center)
    e = [zero + 1.0, zero, zero, zero]
    d = [1.0 / center, zero, zero, zero]
    total = list(d)
    for _ in range(3):
        e = [e[0]] + [e[i] - d[i - 1] for i in range(1, 4)]
        rho_next = 1.0 / (2.0 * sigma - rho)
        d = [rho_next * rho * d[i] + (2.0 * rho_next / spread) * e[i] for i in range(4)]
        total = [a + b for a, b in zip(total, d)]
        rho = rho_next
    total = [jnp.concatenate([c] * (cw // 128), axis=1) for c in total]

    pltpu.make_async_copy(zrecv, zrecv, z_sem.at[0]).wait()
    for k in range(n_gy):
        x = warm[:, cw * k : cw * k + cw]
        for j in range(4):
            x = x + total[j] * zrecv[k, j]
        warmbuf[:, cw * k : cw * k + cw] = x
    puts[3].start()

    for copy in first + second:
        copy.wait_send()
    spread_sent(tsend, trecv, t_sem)
    remote(
        asend.at[pl.ds(0, n_gy - 1)], arecv.at[pl.ds(0, n_gy - 1)], a_sem.at[1], a_sem.at[0],
        (gx, right),
    ).wait_send()
    for copy in coarse_rows:
        copy.wait_send()
    part = pl.ds(0, n_gy - 1)
    remote(zsend.at[part], zrecv.at[part], z_sem.at[1], z_sem.at[0], (gx, right)).wait_send()
    remote(mrecv, mrecv, m_sem.at[1], m_sem.at[0], (gx, right)).wait_send()
    for copy in puts:
        copy.wait()


def put_out(*refs):
    src, dst, via, (isem, osem) = refs[0:4], refs[4:8], refs[8:12], refs[12:14]
    into = [pltpu.make_async_copy(src[i], via[i], isem.at[i]) for i in range(4)]
    out = [pltpu.make_async_copy(via[i], dst[i], osem.at[i]) for i in range(4)]
    for copy in into:
        copy.start()
    for i in range(4):
        into[i].wait()
        out[i].start()
    for copy in out:
        copy.wait()


def per_device(n_gx, n_gy, shift, speed, level, mark, warm, store, film, bath):
    _, hh, ww = shift.shape
    rpd, _ = warm.shape
    cw, ch = ww // 2, hh // 2
    wide, fwide = cw + 128, ww + 128
    crows, frows = ch + 16, hh + 2 * HALO
    nsl = n_gy + 2 * (HALO // rpd)
    vm = lambda *s: pltpu.VMEM(s, F32)
    dma = lambda n: pltpu.SemaphoreType.DMA((n,))
    hbm = pl.BlockSpec(memory_space=pltpu.HBM)
    outs = pl.pallas_call(
        functools.partial(kernel, n_gx, n_gy),
        out_shape=(
            jax.ShapeDtypeStruct(shift.shape, F32),
            jax.ShapeDtypeStruct(speed.shape, F32),
            jax.ShapeDtypeStruct(level.shape, jnp.bfloat16),
            jax.ShapeDtypeStruct(warm.shape, F32),
        ),
        in_specs=[hbm] * 3 + [pl.BlockSpec(memory_space=pltpu.SMEM)] + [hbm] * 4,
        out_specs=(hbm,) * 4,
        scratch_shapes=[
            vm(n_gy, rpd, wide),
            vm(nsl, rpd, wide),
            vm(n_gy, 2, rpd, wide),
            vm(n_gy, 2, rpd, wide),
            vm(hh, 128),
            vm(hh, 128),
            vm(frows, 128),
            vm(frows, 128),
            vm(2, 8, 128),
            vm(2, 8, 128),
            vm(2, 6, 8, ww),
            vm(2, 6, 8, ww),
            vm(2, 6, 8, fwide),
            vm(SUBSTEPS, 4, 8, fwide),
            pltpu.VMEM(level.shape, level.dtype),
            vm(*warm.shape),
            vm(*warm.shape),
            vm(*warm.shape),
            vm(*warm.shape),
            vm(6, frows, fwide),
            vm(frows, fwide),
            vm(frows, fwide),
            vm(frows, fwide),
            vm(crows, wide),
            vm(2, crows, wide),
            vm(wide // 128, frows, 128),
            vm(ww // 128, hh, 128),
            vm(ch, cw),
            vm(2, 8, cw),
            vm(crows, 128),
            vm(crows, 128),
            vm(n_gy, 4, rpd, cw),
            vm(n_gy, 4, rpd, cw),
            vm(1, 128),
            vm(n_gx * n_gy - 1, 1, 128),
            dma(10),
            dma(10),
            dma(4),
            dma(6),
            dma(8),
            dma(8),
            dma(2),
            dma(2),
            dma(7),
            pltpu.VMEM(level.shape, jnp.bfloat16),
            vm(*warm.shape),
            dma(4),
        ],
        compiler_params=pltpu.CompilerParams(
            collective_id=0, has_side_effects=True
        ),
    )(shift, speed, level, mark.reshape(1, hh // SR), warm, store, film, bath)
    return pl.pallas_call(
        put_out,
        out_shape=tuple(jax.ShapeDtypeStruct(o.shape, o.dtype) for o in outs),
        in_specs=[hbm] * 4,
        out_specs=(hbm,) * 4,
        scratch_shapes=[pltpu.VMEM(o.shape, o.dtype) for o in outs] + [dma(4), dma(4)],
    )(*outs)


def solution(mesh):
    rows = P(("gx", "gy"), None)
    plate = P(None, "gx", "gy")
    return jax.shard_map(
        functools.partial(per_device, mesh.shape["gx"], mesh.shape["gy"]),
        mesh=mesh,
        in_specs=(plate, plate, plate, P("gx", "gy"), rows, rows, rows, rows),
        out_specs=(plate, plate, plate, rows),
        check_vma=False,
    )
```

profile of v0, /device:TPU:0, one launch (start us, length us, event | category | flops | bytes accessed | tf_op | source)
XLA Modules:
  0.0 33.0 jit_solution(1031362720180560012)
XLA Ops:
  0.6 30.5 %shard_map.111 = (f32[2,64,512]{2,1,0:T(8,128)}, f32[2,64,512]{2,1,0:T(8,128)}, bf16[2,64,512]{2,1,0:T(8,128)(2,1)}, f32[4,2048]{1,0:T(4,128)}) custom-call(f32[2,64,512]{2,1,0:T(8,128)} %shift.1, f32[2,64,512]{2,1,0:T(8,128)} %speed.1, s32[2,64,512]{2,1,0:T(8,128)} %level_h.1, s32[1,8]{1,0:T(1,128)} %bitcast.1, f32[4,2048]{1,0:T(4,128)} %warm_h.1, ...), custom_call_target="tpu_custom_call" | custom-call | tf_op jit(solution)/shard_map/pallas_call | solution.py:621
  31.1 1.9 %shard_map.112 = (f32[2,64,512]{2,1,0:T(8,128)}, f32[2,64,512]{2,1,0:T(8,128)}, bf16[2,64,512]{2,1,0:T(8,128)(2,1)}, f32[4,2048]{1,0:T(4,128)}) custom-call(f32[2,64,512]{2,1,0:T(8,128)} %get-tuple-element.8.refs_0_, f32[2,64,512]{2,1,0:T(8,128)} %get-tuple-element.9.refs_1_, bf16[2,64,512]{2,1,0:T(8,128)(2,1)} %get-tuple-element.10.refs_2_, ...), custom_call_target="tpu_custom_call" | custom-call | tf_op jit(solution)/shard_map/pallas_call | solution.py:684
where the time goes:
time: 33.2 us; the launch traced here: 33 us
  Pallas kernels  32.3 us (97%)
  between operations  0.64 us (2%)
    pallas_call x1, Pallas kernels, per_device(): pl.pallas_call(functools.partial(kernel, n_gx, n_gy), out_shape=(jax.Shap...  30.5 us
    pallas_call x1, Pallas kernels, per_device(): pl.pallas_call(put_out, out_shape=tuple((jax.ShapeDtypeStruct(o.shape, o....  1.85 us

commit v1 on v0

--- a/solution.py
+++ b/solution.py
@@ -33,7 +33,7 @@
     shift,
     speed,
     level_h,
-    mark,
+    mark_h,
     warm_h,
     store_h,
     film_h,
@@ -86,9 +86,7 @@
     z_sem,
     m_sem,
     in_sem,
-    dambuf,
-    warmbuf,
-    out_sem,
+    mark,
 ):
     ndev = n_gx * n_gy
     gx = lax.axis_index("gx")
@@ -105,6 +103,15 @@
     left = lax.rem(gy + n_gy - 1, n_gy)
     right = lax.rem(gy + 1, n_gy)
 
+    barrier = pltpu.get_barrier_semaphore()
+
+    def greet(k, c):
+        t = lax.rem(me + k, ndev)
+        pl.semaphore_signal(barrier, inc=1, device_id=(t // n_gy, t % n_gy), device_id_type=MESH)
+        return c
+
+    lax.fori_loop(1, ndev, greet, 0)
+
     own_r = slice(HALO, HALO + hh)
     loads = [
         pltpu.make_async_copy(src, dst, in_sem.at[i])
@@ -117,21 +124,15 @@
                 (store_h, store),
                 (film_h, film),
                 (bath_h, bath),
+                (mark_h, mark),
             )
         )
     ]
     for copy in loads:
         copy.start()
-    barrier = pltpu.get_barrier_semaphore()
-
-    def greet(k, c):
-        t = lax.rem(me + k, ndev)
-        pl.semaphore_signal(barrier, inc=1, device_id=(t // n_gy, t % n_gy), device_id_type=MESH)
-        return c
-
-    lax.fori_loop(1, ndev, greet, 0)
 
     lane = lane_iota((hh, 128))
+    loads[7].wait()
     for s in range(hh // SR):
         wt[HALO + SR * s : HALO + SR * s + SR, 0:ww] = jnp.full((SR, ww), mark[0, s], jnp.int32).astype(F32)
     w_own = wt[own_r, 0:ww]
@@ -262,7 +263,7 @@
             remote(send, recv.at[whole], sem.at[3], sem.at[0], (down, gy)).wait_send()
 
     spread_out(tsend, trecv, t_sem)
-    for copy in first:
+    for copy in first[2:8] + first[8:10] + first[0:2]:
         copy.start()
 
     pltpu.make_async_copy(trecv, trecv, t_sem.at[0]).wait()
@@ -470,21 +471,10 @@
     for copy in second:
         copy.start()
 
-    dambuf[0] = dam_x.astype(jnp.bfloat16)
-    dambuf[1] = dam_y.astype(jnp.bfloat16)
-    puts = [
-        pltpu.make_async_copy(src, dst, out_sem.at[i])
-        for i, (src, dst) in enumerate(
-            (
-                (state.at[0:2, own_r, 0:ww], o_shift),
-                (state.at[2:4, own_r, 0:ww], o_speed),
-                (dambuf, o_dam),
-                (warmbuf, o_warm),
-            )
-        )
-    ]
-    for copy in puts[0:3]:
-        copy.start()
+    o_dam[0] = dam_x.astype(jnp.bfloat16)
+    o_dam[1] = dam_y.astype(jnp.bfloat16)
+    o_shift[...] = state[0:2, own_r, 0:ww]
+    o_speed[...] = state[2:4, own_r, 0:ww]
 
     for copy in coarse_rows:
         copy.wait_recv()
@@ -521,7 +511,8 @@
     ]
     offsum = faces[0] + faces[1] + faces[2] + faces[3]
     diagonal = acf[0] + offsum
-    ratio = offsum / diagonal
+    inv = 1.0 / diagonal
+    ratio = offsum * inv
     peak = jnp.max(ratio[8 : 8 + ch, 0:cw])
     msend[...] = jnp.full((1, 128), peak, F32)
 
@@ -536,8 +527,8 @@
 
     t_all = tc[...]
     near = sum(f * nb for f, nb in zip(faces, four(t_all)))
-    z = (acf[1] - (diagonal * t_all - near)) / diagonal
-    faces = [f / diagonal for f in faces]
+    z = (acf[1] - (diagonal * t_all - near)) * inv
+    faces = [f * inv for f in faces]
     for j in range(4):
         if j:
             z = z - sum(f * nb for f, nb in zip(faces, four(z)))
@@ -576,8 +567,7 @@
         x = warm[:, cw * k : cw * k + cw]
         for j in range(4):
             x = x + total[j] * zrecv[k, j]
-        warmbuf[:, cw * k : cw * k + cw] = x
-    puts[3].start()
+        o_warm[:, cw * k : cw * k + cw] = x
 
     for copy in first + second:
         copy.wait_send()
@@ -591,19 +581,13 @@
     part = pl.ds(0, n_gy - 1)
     remote(zsend.at[part], zrecv.at[part], z_sem.at[1], z_sem.at[0], (gx, right)).wait_send()
     remote(mrecv, mrecv, m_sem.at[1], m_sem.at[0], (gx, right)).wait_send()
-    for copy in puts:
-        copy.wait()
 
 
 def put_out(*refs):
-    src, dst, via, (isem, osem) = refs[0:4], refs[4:8], refs[8:12], refs[12:14]
-    into = [pltpu.make_async_copy(src[i], via[i], isem.at[i]) for i in range(4)]
-    out = [pltpu.make_async_copy(via[i], dst[i], osem.at[i]) for i in range(4)]
-    for copy in into:
+    src, dst, sem = refs[0:4], refs[4:8], refs[8]
+    out = [pltpu.make_async_copy(src[i], dst[i], sem.at[i]) for i in range(4)]
+    for copy in out:
         copy.start()
-    for i in range(4):
-        into[i].wait()
-        out[i].start()
     for copy in out:
         copy.wait()
 
@@ -621,13 +605,13 @@
     outs = pl.pallas_call(
         functools.partial(kernel, n_gx, n_gy),
         out_shape=(
-            jax.ShapeDtypeStruct(shift.shape, F32),
-            jax.ShapeDtypeStruct(speed.shape, F32),
-            jax.ShapeDtypeStruct(level.shape, jnp.bfloat16),
-            jax.ShapeDtypeStruct(warm.shape, F32),
+            pltpu.VMEM(shift.shape, F32),
+            pltpu.VMEM(speed.shape, F32),
+            pltpu.VMEM(level.shape, jnp.bfloat16),
+            pltpu.VMEM(warm.shape, F32),
         ),
-        in_specs=[hbm] * 3 + [pl.BlockSpec(memory_space=pltpu.SMEM)] + [hbm] * 4,
-        out_specs=(hbm,) * 4,
+        in_specs=[hbm] * 8,
+        out_specs=(pl.BlockSpec(memory_space=pltpu.VMEM),) * 4,
         scratch_shapes=[
             vm(n_gy, rpd, wide),
             vm(nsl, rpd, wide),
@@ -672,10 +656,8 @@
             dma(8),
             dma(2),
             dma(2),
-            dma(7),
-            pltpu.VMEM(level.shape, jnp.bfloat16),
-            vm(*warm.shape),
-            dma(4),
+            dma(8),
+            pltpu.SMEM((1, hh // SR), mark.dtype),
         ],
         compiler_params=pltpu.CompilerParams(
             collective_id=0, has_side_effects=True
@@ -684,10 +666,10 @@
     return pl.pallas_call(
         put_out,
         out_shape=tuple(jax.ShapeDtypeStruct(o.shape, o.dtype) for o in outs),
-        in_specs=[hbm] * 4,
+        in_specs=[pl.BlockSpec(memory_space=pltpu.VMEM)] * 4,
         out_specs=(hbm,) * 4,
-        scratch_shapes=[pltpu.VMEM(o.shape, o.dtype) for o in outs] + [dma(4), dma(4)],
-    )(*outs)
+        scratch_shapes=[dma(4)],
+    )(*(pltpu.with_memory_space_constraint(o, pltpu.VMEM) for o in outs))
 
 
 def solution(mesh):

time: 33.2 us -> 30.1 us (0.907)
  Pallas kernels: 32.3 us -> 29.2 us
    pallas_call x1, Pallas kernels: 30.5 us -> 28.4 us  [per_device(): pl.pallas_call(functools.partial(kernel, n_gx, n_gy), out_shape=(pltpu.VM...]
    pallas_call x1, Pallas kernels: 1.85 us -> 0.87 us  [per_device(): pl.pallas_call(put_out, out_shape=tuple((jax.ShapeDtypeStruct(o.shape, o....]
where the time goes in v1:
time: 30.1 us; the launch traced here: 29.9 us
  Pallas kernels  29.2 us (97%)
  between operations  0.64 us (2%)
    pallas_call x1, Pallas kernels, per_device(): pl.pallas_call(functools.partial(kernel, n_gx, n_gy), out_shape=(pltpu.VM...  28.4 us
    pallas_call x1, Pallas kernels, per_device(): pl.pallas_call(put_out, out_shape=tuple((jax.ShapeDtypeStruct(o.shape, o....  0.87 us

profile of v1, /device:TPU:0, one launch (start us, length us, event | category | flops | bytes accessed | tf_op | source)
XLA Modules:
  0.0 29.9 jit_solution(5589131585507242628)
XLA Ops:
  0.6 28.4 %shard_map.111 = (f32[2,64,512]{2,1,0:T(8,128)S(1)}, f32[2,64,512]{2,1,0:T(8,128)S(1)}, bf16[2,64,512]{2,1,0:T(8,128)(2,1)S(1)}, f32[4,2048]{1,0:T(4,128)S(1)}) custom-call(f32[2,64,512]{2,1,0:T(8,128)} %shift.1, f32[2,64,512]{2,1,0:T(8,128)} %speed.1, s32[2,64,512]{2,1,0:T(8,128)} %level_h.1, s32[1,8]{1,0:T(1,128)} %bitcast.1, f32[4,2048]{1,0:T(4,128)} %warm_h.1, ...), custom_call_target="tpu_custom_call" | custom-call | tf_op jit(solution)/shard_map/pallas_call | solution.py:605
  29.0 0.9 %shard_map.112 = (f32[2,64,512]{2,1,0:T(8,128)}, f32[2,64,512]{2,1,0:T(8,128)}, bf16[2,64,512]{2,1,0:T(8,128)(2,1)}, f32[4,2048]{1,0:T(4,128)}) custom-call(f32[2,64,512]{2,1,0:T(8,128)S(1)} %get-tuple-element.8.refs_0_, f32[2,64,512]{2,1,0:T(8,128)S(1)} %get-tuple-element.9.refs_1_, bf16[2,64,512]{2,1,0:T(8,128)(2,1)S(1)} %get-tuple-element.10.refs_2_, ...), custom_call_target="tpu_custom_call" | custom-call | tf_op jit(solution)/shard_map/pallas_call | solution.py:666

commit v2 on v1

v2 whole, which is shorter than its diff:
```python
import functools
import math

import jax
import jax.numpy as jnp
from jax import lax
from jax.experimental import pallas as pl
from jax.experimental.pallas import tpu as pltpu
from jax.sharding import PartitionSpec as P

SR = 8
SEG = 128
SUBSTEPS = 8
HALO = 8
FIELDS = 7
MESH = pl.DeviceIdType.MESH
F32 = jnp.float32


def lane_iota(shape):
    return lax.broadcasted_iota(jnp.int32, shape, 1)


def row_iota(shape):
    return lax.broadcasted_iota(jnp.int32, shape, 0)


def full_dot(a, b):
    return jnp.dot(a, b, precision=lax.Precision.HIGHEST, preferred_element_type=F32)


def pick(x, index):
    return jnp.take_along_axis(x, index, axis=1)


def kernel(
    n_gx,
    n_gy,
    shift,
    speed,
    level_h,
    mark_h,
    warm_h,
    store_h,
    film_h,
    bath_h,
    su,
    o_speed,
    o_dam,
    o_warm,
    tsend,
    trecv,
    asend,
    arecv,
    pk,
    rk,
    ck,
    rowsend,
    rowrecv,
    keep,
    hist_n,
    hist_u,
    level,
    warm,
    store,
    film,
    bath,
    sv,
    ss,
    kw,
    kh,
    tx,
    ty,
    fine,
    nx,
    tcx,
    acf,
    widebuf,
    tab_s,
    gap,
    cbuf,
    crow,
    ccl,
    ccr,
    zsend,
    zrecv,
    msend,
    mrecv,
    n_send,
    n_recv,
    t_sem,
    far_sem,
    a_sem,
    c_send,
    c_recv,
    z_sem,
    m_sem,
    in_sem,
    mark,
):
    ndev = n_gx * n_gy
    gx = lax.axis_index("gx")
    gy = lax.axis_index("gy")
    me = gx * n_gy + gy
    _, hh, ww = shift.shape
    rpd, _ = warm_h.shape
    cw = ww // 2
    ch = hh // 2
    hb = HALO // rpd
    nsl = n_gy + 2 * hb
    nt = ww // 128
    ntile = nt + 1
    nct = cw // 128
    frows = hh + 2 * HALO
    nstrip = frows // 8
    up = lax.rem(gx + n_gx - 1, n_gx)
    down = lax.rem(gx + 1, n_gx)
    left = lax.rem(gy + n_gy - 1, n_gy)
    right = lax.rem(gy + 1, n_gy)
    has_u, has_d = gx > 0, gx < n_gx - 1
    has_l, has_r = gy > 0, gy < n_gy - 1
    own_r = slice(HALO, HALO + hh)

    barrier = pltpu.get_barrier_semaphore()
    warm_load = pltpu.make_async_copy(warm_h, warm, in_sem.at[0])
    warm_load.start()

    def greet(a, b):
        pl.semaphore_signal(barrier, inc=1, device_id=(a, b), device_id_type=MESH)

    for k in range(1, n_gy):
        greet(gx, lax.rem(gy + k, n_gy))
    for k in range(1, n_gx):
        greet(lax.rem(gx + k, n_gx), gy)
    for a in (up, down):
        for b in (left, right):
            greet(a, b)

    loads = [
        pltpu.make_async_copy(src, dst, in_sem.at[i])
        for i, (src, dst) in enumerate(
            (
                (mark_h, mark),
                (level_h, level),
                (store_h, store),
                (film_h, film),
                (bath_h, bath),
            ),
            1,
        )
    ]
    loads[0].start()
    loads[1].start()
    for src, dst, i in ((shift, su, 6), (speed, sv, 7)):
        for t in range(nt):
            pltpu.make_async_copy(
                src.at[:, :, 128 * t : 128 * t + 128], dst.at[:, t, own_r, :], in_sem.at[i]
            ).start()
    for copy in loads[2:]:
        copy.start()

    def loaded(dst, i):
        part = dst.at[:, 0:nt, own_r, :]
        pltpu.make_async_copy(part, part, in_sem.at[i]).wait()

    lane_c = lane_iota((rpd, 128))

    def chunk(value, k):
        after = value[:, (cw * (k + 1)) % (cw * n_gy) :][:, 0:128]
        before = value[:, (cw * k - 128) % (cw * n_gy) :][:, 0:128]
        return value[:, cw * k : cw * k + cw], jnp.where(lane_c < 64, after, before)

    def remote(src, dst, ssem, rsem, where):
        return pltpu.make_async_remote_copy(
            src_ref=src, dst_ref=dst, send_sem=ssem, recv_sem=rsem, device_id=where,
            device_id_type=MESH,
        )

    warm_load.wait()
    t_own = warm[...]
    for k in range(n_gy):
        main, edge = chunk(t_own, k)
        tsend[k, :, 0:cw] = main
        tsend[k, :, cw : cw + 128] = edge

    pl.semaphore_wait(barrier, n_gy + n_gx + 2)

    def along(k, c):
        t = lax.rem(gy + k, n_gy)
        remote(tsend.at[t], trecv.at[gy + hb], t_sem.at[1], t_sem.at[0], (gx, t)).start()
        return c

    lax.fori_loop(1, n_gy, along, 0)
    pltpu.make_async_copy(tsend.at[gy], trecv.at[gy + hb], t_sem.at[0]).start()

    sharp = -4.0 * math.log2(math.e)
    lane = lane_iota((hh, 128))
    loads[0].wait()
    for s in range(hh // SR):
        kw[HALO + SR * s : HALO + SR * s + SR, :] = (
            jnp.full((SR, 128), mark[0, s], jnp.int32).astype(F32) * sharp
        )
    w_own = kw[own_r, :] * (0.125 / sharp)
    grow = gx * hh + row_iota((hh, 128))
    loads[1].wait()
    for t in range(nt):
        cols = slice(128 * t, 128 * t + 128)
        gcol = gy * ww + 128 * t + lane
        ss[0, t, own_r, :] = jnp.where(grow >= 1, 1.0 - level[0, :, cols].astype(F32) * w_own, 0.0)
        ss[1, t, own_r, :] = jnp.where(gcol >= 1, 1.0 - level[1, :, cols].astype(F32) * w_own, 0.0)
    loaded(su, 6)
    loaded(sv, 7)
    for c in range(2):
        for t in range(nt):
            sv[c, t, own_r, :] = 0.4 * sv[c, t, own_r, :]
    acc_l = jnp.zeros((hh, 128), F32)
    acc_r = jnp.zeros((hh, 128), F32)
    fields = [(ref, c) for ref in (su, sv, ss) for c in range(2)]
    for f in range(FIELDS):
        if f < 6:
            ref, c = fields[f]
            first, last = ref[c, 0, own_r, :], ref[c, nt - 1, own_r, :]
        else:
            first = last = kw[own_r, :]
        here = (lane >= 8 * f) & (lane < 8 * f + 8)
        first = pltpu.roll(first, 8 * f, 1) if f else first
        acc_l = jnp.where(here, first, acc_l)
        acc_r = jnp.where(here, pltpu.roll(last, 8 * f + 8, 1), acc_r)
    pk[0] = acc_l
    pk[1] = acc_r
    side_l = remote(pk.at[0], rk.at[1], n_send.at[0], n_recv.at[1], (gx, left))
    side_r = remote(pk.at[1], rk.at[0], n_send.at[1], n_recv.at[0], (gx, right))
    top, end = slice(0, 8), slice(hh - 8, hh)
    corners = [
        (has_u & has_l, remote(pk.at[0, top], ck.at[3], n_send.at[2], n_recv.at[5], (up, left)), 2),
        (has_u & has_r, remote(pk.at[1, top], ck.at[2], n_send.at[3], n_recv.at[4], (up, right)), 3),
        (has_d & has_l, remote(pk.at[0, end], ck.at[1], n_send.at[4], n_recv.at[3], (down, left)), 4),
        (has_d & has_r, remote(pk.at[1, end], ck.at[0], n_send.at[5], n_recv.at[2], (down, right)), 5),
    ]
    rows_u = remote(rowsend.at[0], rowrecv.at[1], n_send.at[6], n_recv.at[7], (up, gy))
    rows_d = remote(rowsend.at[1], rowrecv.at[0], n_send.at[7], n_recv.at[6], (down, gy))
    sends = [(has_l, side_l), (has_r, side_r)] + [(a, b) for a, b, _ in corners]
    sends += [(has_u, rows_u), (has_d, rows_d)]

    def start_if(cond, copy):
        @pl.when(cond)
        def _():
            copy.start()

    def sent_if(cond, copy):
        @pl.when(cond)
        def _():
            copy.wait_send()

    def came_if(cond, copy):
        @pl.when(cond)
        def _():
            copy.wait_recv()

    for cond, copy in sends[0:6]:
        start_if(cond, copy)
    for side, at in ((0, HALO), (1, HALO + hh - 8)):
        for f, (ref, c) in enumerate(fields):
            for t in range(nt):
                rowsend[side, nt * f + t] = ref[c, t, at : at + 8, :]
        rowsend[side, 6 * nt] = kw[at : at + 8, :]
    for cond, copy in sends[6:8]:
        start_if(cond, copy)

    k_i, n_i = row_iota((256, 128)), lane_iota((256, 128))
    pos = (k_i % SEG).astype(F32)
    col = (2 * (n_i % 64)).astype(F32)
    tab = jnp.exp(jnp.abs(pos - col) * (-4.0 / SEG)) + jnp.exp(jnp.abs(pos - col - 1.0) * (-4.0 / SEG))
    tab_s[...] = jnp.where(k_i // SEG == n_i // 64, tab * (1.0 / SEG), 0.0)
    for i in (2, 3, 4):
        loads[i].wait()
    base = store[...] + film[...]
    force_own = store[...] * t_own + film[...] * bath[...]
    for k in range(n_gy):
        for q, val in enumerate((base, force_own)):
            main, edge = chunk(val, k)
            asend[k, q, :, 0:cw] = main
            asend[k, q, :, cw : cw + 128] = edge
    for strip in ((nstrip - 2) * 8, nstrip * 8):
        nx[:, :, strip : strip + 8, :] = jnp.zeros((2, ntile, 8, 128), F32)
    keeps = (slice(16, 24), slice(frows - 24, frows - 16))
    for i, rows in enumerate(keeps):
        for f, (ref, c) in enumerate(fields):
            for t in range(nt):
                keep[i, f, t] = ref[c, t, rows, :]

    mid = trecv.at[pl.ds(hb, n_gy)]
    pltpu.make_async_copy(mid, mid, t_sem.at[0]).wait()
    far_u = remote(
        trecv.at[pl.ds(hb, hb)], trecv.at[pl.ds(hb + n_gy, hb)], t_sem.at[2], far_sem.at[1], (up, gy)
    )
    far_d = remote(
        trecv.at[pl.ds(n_gy, hb)], trecv.at[pl.ds(0, hb)], t_sem.at[3], far_sem.at[0], (down, gy)
    )
    start_if(has_u, far_u)
    start_if(has_d, far_d)

    def late(k, c):
        t = lax.rem(gy + k, n_gy)
        remote(asend.at[t], arecv.at[gy], a_sem.at[1], a_sem.at[0], (gx, t)).start()
        return c

    lax.fori_loop(1, n_gy, late, 0)
    pltpu.make_async_copy(asend.at[gy], arecv.at[gy], a_sem.at[0]).start()
    crows = ch + 16
    wide = cw + 128
    lane8 = lane_iota((8, 128))
    first_lane, last_lane = lane8 == 0, lane8 == 127

    def close_edge(rows):
        edge = tcx[nct, rows, :]
        edge = jnp.where(~has_l & last_lane, pltpu.roll(tcx[0, rows, :], 127, 1), edge)
        edge = jnp.where(~has_r & first_lane, pltpu.roll(tcx[nct - 1, rows, :], 1, 1), edge)
        tcx[nct, rows, :] = edge

    for k in range(hb, hb + n_gy):
        for j in range(nct + 1):
            tcx[j, rpd * k : rpd * k + rpd, :] = trecv[k, :, 128 * j : 128 * j + 128]
    for c in range(8, 8 + ch, 8):
        close_edge(slice(c, c + 8))
    half = lane8 // 2
    step = jnp.where(lane8 % 2 == 0, -1, 1)
    lo_g, lo_h = half, jnp.maximum(half + step, 0)
    hi_g, hi_h = half + 64, jnp.minimum(half + 64 + step, 127)
    ed_g = jnp.where(lane8 < 64, half, half + 64)
    ed_h = jnp.minimum(jnp.maximum(ed_g + step, 0), 127)

    def before(tiles):
        turned = [pltpu.roll(x, 1, 1) for x in tiles]
        return [jnp.where(first_lane, turned[t - 1], turned[t]) for t in range(len(tiles))]

    def after(tiles):
        turned = [pltpu.roll(x, 127, 1) for x in tiles]
        n = len(tiles)
        return [jnp.where(last_lane, turned[(t + 1) % n], turned[t]) for t in range(n)]

    def above(ref, s):
        return ref[8 * s - 1 : 8 * s + 7, :] if s else pltpu.roll(ref[0:8, :], 1, 0)

    def heat_x(s):
        rows = slice(8 * s, 8 * s + 8)
        for t in range(ntile):
            tx[t, rows, :] = 0.3 * (fine[t, rows, :] + above(fine.at[t], s))

    def prolong(p):
        c = 8 * p + 4
        for j in range(nct + 1):
            here = 0.75 * tcx[j, c : c + 8, :]
            widebuf[j, pl.ds(16 * p, 8, stride=2), :] = here + 0.25 * tcx[j, c - 1 : c + 7, :]
            widebuf[j, pl.ds(16 * p + 1, 8, stride=2), :] = here + 0.25 * tcx[j, c + 1 : c + 9, :]
        for s in (2 * p, 2 * p + 1):
            rows = slice(8 * s, 8 * s + 8)
            r = [widebuf[j, rows, :] for j in range(nct + 1)]
            fwd = [pltpu.roll(x, 1, 1) for x in r]
            bwd = [pltpu.roll(x, 127, 1) for x in r]
            f = []
            for j in range(nct):
                f.append(
                    0.75 * pick(r[j], lo_g)
                    + 0.25 * jnp.where(first_lane, fwd[j - 1], pick(r[j], lo_h))
                )
                f.append(
                    0.75 * pick(r[j], hi_g)
                    + 0.25 * jnp.where(last_lane, bwd[j + 1], pick(r[j], hi_h))
                )
            e = pick(r[nct], ed_h)
            e = jnp.where(first_lane, fwd[nct - 1], jnp.where(last_lane, bwd[0], e))
            f.append(0.75 * pick(r[nct], ed_g) + 0.25 * e)
            prev = before(f)
            for t in range(ntile):
                fine[t, rows, :] = f[t]
                ty[t, rows, :] = 0.3 * (f[t] + prev[t])

    npair = nstrip // 2
    for p in range(1, npair - 1):
        prolong(p)
    for s in range(2, nstrip - 2):
        heat_x(s)

    came_if(has_l, side_r)
    came_if(has_r, side_l)

    def unpack(got_l, got_r, rows, outside):
        shape = got_l.shape
        lanes = lane_iota(shape)
        gone = outside | (~has_l & (lanes >= 64)) | (~has_r & (lanes < 64))
        for f in range(FIELDS):
            from_r = pltpu.roll(got_r, 128 - 8 * f, 1) if f else got_r
            from_l = pltpu.roll(got_l, 120 - 8 * f, 1)
            side = jnp.where(lanes < 8, from_r, jnp.where(lanes >= 120, from_l, 0.0))
            side = jnp.where(gone, 0.0, side)
            if f < 6:
                ref, c = fields[f]
                ref[c, nt, rows, :] = side
            else:
                kh[rows, :] = side

    unpack(rk[0], rk[1], own_r, False)
    for i, rows in enumerate(keeps):
        for f, (ref, c) in enumerate(fields):
            keep[i, f, nt] = ref[c, nt, rows, :]

    def edges(s):
        rows = slice(8 * s, 8 * s + 8)
        u0 = [su[0, t, rows, :] for t in range(ntile)]
        u1 = [su[1, t, rows, :] for t in range(ntile)]
        k_main, k_side = kw[rows, :], kh[rows, :]
        b0, b1 = before(u0), before(u1)
        ay, ny = [], []
        for t in range(ntile):
            k = k_main if t < nt else k_side
            open_x = u0[t] - above(su.at[0, t], s) - tx[t, rows, :]
            st = jnp.maximum(open_x, 0.0)
            sp = jnp.minimum(ss[0, t, rows, :], jnp.exp2(st * st * k))
            ss[0, t, rows, :] = sp
            nx[0, t, rows, :] = sp * open_x
            nx[1, t, rows, :] = sp * (u1[t] - above(su.at[1, t], s))
            open_y = u1[t] - b1[t] - ty[t, rows, :]
            st = jnp.maximum(open_y, 0.0)
            sp = jnp.minimum(ss[1, t, rows, :], jnp.exp2(st * st * k))
            ss[1, t, rows, :] = sp
            ny.append(sp * open_y)
            ay.append(sp * (u0[t] - b0[t]))
        fy0 = [a - b for a, b in zip(after(ay), ay)]
        fy1 = [a - b for a, b in zip(after(ny), ny)]
        return fy0, fy1

    def advance(s, fy):
        rows = slice(8 * s, 8 * s + 8)
        below = slice(8 * s + 1, 8 * s + 9)
        for c in range(2):
            for t in range(ntile):
                force = (nx[c, t, below, :] - nx[c, t, rows, :]) + fy[c][t]
                v = 0.98 * sv[c, t, rows, :] + 0.16 * force
                sv[c, t, rows, :] = v
                su[c, t, rows, :] = su[c, t, rows, :] + v

    def interior(i, carry):
        old = None
        for s in range(2, nstrip - 2):
            if s == nstrip - 4:
                for c in range(2):
                    for t in range(ntile):
                        hist_u[i, c, t] = su[c, t, 8 * s : 8 * s + 8, :]
            new = edges(s)
            if s == 3:
                for c in range(2):
                    for t in range(ntile):
                        hist_n[i, c, t] = nx[c, t, 8 * s : 8 * s + 8, :]
            if old:
                advance(s - 1, old)
            old = new
        advance(nstrip - 3, old)
        return carry

    lax.fori_loop(0, SUBSTEPS, interior, 0)

    for side, (here, at, slot, line) in enumerate(
        ((has_u, 0, 0, 8), (has_d, ch + 8, hb + n_gy, ch + 7))
    ):
        came_if(here, far_u if side else far_d)

        @pl.when(here)
        def _():
            for k in range(hb):
                for j in range(nct + 1):
                    tcx[j, at + rpd * k : at + rpd * k + rpd, :] = trecv[
                        slot + k, :, 128 * j : 128 * j + 128
                    ]
            close_edge(slice(at, at + 8))

        @pl.when(jnp.logical_not(here))
        def _():
            for j in range(nct + 1):
                tcx[j, at : at + 8, :] = jnp.broadcast_to(tcx[j, line : line + 1, :], (8, 128))

    prolong(0)
    prolong(npair - 1)
    for s in (0, 1, 2, nstrip - 2, nstrip - 1):
        heat_x(s)

    came_if(has_u & has_l, corners[3][1])
    came_if(has_u & has_r, corners[2][1])
    came_if(has_d & has_l, corners[1][1])
    came_if(has_d & has_r, corners[0][1])
    came_if(has_u, rows_d)
    came_if(has_d, rows_u)
    for side, (here, at) in enumerate(((has_u, 0), (has_d, hh + HALO))):
        rows = slice(at, at + 8)
        for f, (ref, c) in enumerate(fields):
            for t in range(nt):
                ref[c, t, rows, :] = jnp.where(here, rowrecv[side, nt * f + t], 0.0)
        kw[rows, :] = jnp.where(here, rowrecv[side, 6 * nt], 0.0)
        unpack(ck[2 * side], ck[2 * side + 1], rows, ~here)
    for i, rows in enumerate(keeps):
        for f, (ref, c) in enumerate(fields):
            for t in range(ntile):
                ref[c, t, rows, :] = keep[i, f, t]
    line = frows - 25
    final = [[su[c, t, line : line + 1, :] for t in range(ntile)] for c in range(2)]
    for c in range(2):
        for t in range(ntile):
            hist_n[SUBSTEPS, c, t, 0:1, :] = final[c][t]

    def border(i, carry):
        for c in range(2):
            for t in range(ntile):
                nx[c, t, 24:32, :] = hist_n[i, c, t]
                su[c, t, line : line + 1, :] = hist_u[i, c, t, 7:8, :]
        for at in (0, nstrip - 3):
            old = None
            for s in range(at, at + 3):
                new = edges(s)
                if old:
                    advance(s - 1, old)
                old = new
            advance(at + 2, old)
        return carry

    lax.fori_loop(0, SUBSTEPS, border, 0)
    for c in range(2):
        for t in range(ntile):
            su[c, t, line : line + 1, :] = hist_n[SUBSTEPS, c, t, 0:1, :]

    pltpu.make_async_copy(arecv, arecv, a_sem.at[0]).wait()
    for k in range(n_gy):
        for q in range(2):
            acf[q, 8 + rpd * k : 8 + rpd * k + rpd, :] = arecv[k, q]
    coarse_rows = [
        remote(
            acf.at[:, 8:16], acf.at[:, ch + 8 : ch + 16], a_sem.at[2], a_sem.at[4], (up, gy)
        ),
        remote(acf.at[:, ch : ch + 8], acf.at[:, 0:8], a_sem.at[3], a_sem.at[5], (down, gy)),
    ]
    for copy in coarse_rows:
        copy.start()

    for t in range(nt):
        gcol = gy * ww + 128 * t + lane
        dam_x = jnp.where(grow >= 1, 1.0 - ss[0, t, own_r, :], 0.0)
        dam_y = jnp.where(gcol >= 1, 1.0 - ss[1, t, own_r, :], 0.0)
        gap[t] = dam_x + dam_y
        o_dam[0, t] = dam_x.astype(jnp.bfloat16)
        o_dam[1, t] = dam_y.astype(jnp.bfloat16)
    rows2 = jnp.concatenate(
        [
            gap[t, pl.ds(0, ch, stride=2), :] + gap[t, pl.ds(1, ch, stride=2), :]
            for t in range(ww // 128)
        ],
        axis=1,
    )
    pairs = ww // 256
    glow = full_dot(
        jnp.concatenate([rows2[:, 256 * t : 256 * t + 256] for t in range(pairs)], axis=0), tab_s[...]
    )
    resist = jnp.concatenate([glow[ch * t : ch * t + ch] for t in range(pairs)], axis=1)
    t_all = jnp.concatenate([tcx[j] for j in range(nct + 1)], axis=1)
    cond_own = (1.0 + 0.5 * t_all[8 : 8 + ch, 0:cw]) / (1.0 + resist)
    cbuf[...] = cond_own
    def neighbours(send_l, send_r, row_u, row_d, recv_l, recv_r, got_u, got_d, rows, ssem, rsem):
        top, end = slice(0, 8), slice(rows - 8, rows)
        lo, mid, hi = slice(0, 8), slice(8, rows + 8), slice(rows + 8, rows + 16)
        return [
            remote(row_u, got_d, ssem.at[0], rsem.at[0], (up, gy)),
            remote(row_d, got_u, ssem.at[1], rsem.at[1], (down, gy)),
            remote(send_l, recv_r.at[mid], ssem.at[2], rsem.at[2], (gx, left)),
            remote(send_r, recv_l.at[mid], ssem.at[3], rsem.at[3], (gx, right)),
            remote(send_l.at[top], recv_r.at[hi], ssem.at[4], rsem.at[4], (up, left)),
            remote(send_r.at[top], recv_l.at[hi], ssem.at[5], rsem.at[5], (up, right)),
            remote(send_l.at[end], recv_r.at[lo], ssem.at[6], rsem.at[6], (down, left)),
            remote(send_r.at[end], recv_l.at[lo], ssem.at[7], rsem.at[7], (down, right)),
        ]

    second = neighbours(
        cbuf.at[:, 0:128], cbuf.at[:, cw - 128 : cw], cbuf.at[0:8], cbuf.at[ch - 8 : ch],
        ccl, ccr, crow.at[0], crow.at[1], ch, c_send, c_recv,
    )
    for copy in second:
        copy.start()

    for c in range(2):
        for t in range(nt):
            o_speed[c, t] = 2.5 * sv[c, t, own_r, :]

    for copy in coarse_rows:
        copy.wait_recv()

    for copy in second:
        copy.wait_recv()
    lane_k = lane_iota((crows, 128))
    cond = jnp.concatenate(
        [
            jnp.concatenate([crow[0], cbuf[...], crow[1]], axis=0),
            jnp.where(lane_k < 64, ccr[...], ccl[...]),
        ],
        axis=1,
    )
    crow_i, clane_i = row_iota((crows, wide)), lane_iota((crows, wide))
    crow_g = gx * ch - 8 + crow_i
    ccol_g = gy * cw + jnp.where(clane_i < cw + 64, clane_i, clane_i - wide)

    def four(x):
        return (
            pltpu.roll(x, 1, 0),
            pltpu.roll(x, crows - 1, 0),
            pltpu.roll(x, 1, 1),
            pltpu.roll(x, wide - 1, 1),
        )

    masks = (
        crow_g >= 1,
        crow_g <= ch * n_gx - 2,
        ccol_g >= 1,
        ccol_g <= cw * n_gy - 2,
    )
    faces = [
        jnp.where(m, 0.5 * (cond + nb), 0.0) for m, nb in zip(masks, four(cond))
    ]
    offsum = faces[0] + faces[1] + faces[2] + faces[3]
    diagonal = acf[0] + offsum
    inv = 1.0 / diagonal
    ratio = offsum * inv
    peak = jnp.max(ratio[8 : 8 + ch, 0:cw])
    msend[...] = jnp.full((1, 128), peak, F32)

    def tell(k, c):
        t = lax.rem(me + k, ndev)
        remote(
            msend, mrecv.at[k - 1], m_sem.at[1], m_sem.at[0], (t // n_gy, t % n_gy)
        ).start()
        return c

    lax.fori_loop(1, ndev, tell, 0)

    near = sum(f * nb for f, nb in zip(faces, four(t_all)))
    z = (acf[1] - (diagonal * t_all - near)) * inv
    faces = [f * inv for f in faces]
    for j in range(4):
        if j:
            z = z - sum(f * nb for f, nb in zip(faces, four(z)))
        for k in range(n_gy):
            zsend[k, j] = z[8 + rpd * k : 8 + rpd * k + rpd, 0:cw]

    def home(k, c):
        t = lax.rem(gy + k, n_gy)
        remote(zsend.at[t], zrecv.at[gy], z_sem.at[1], z_sem.at[0], (gx, t)).start()
        return c

    lax.fori_loop(1, n_gy, home, 0)
    pltpu.make_async_copy(zsend.at[gy], zrecv.at[gy], z_sem.at[0]).start()

    pltpu.make_async_copy(mrecv, mrecv, m_sem.at[0]).wait()
    peak = jnp.maximum(jnp.max(mrecv[...], axis=0), msend[...])[0:1, :]
    low, high = 1.0 - peak, 1.0 + peak
    center = 0.5 * (high + low)
    spread = 0.5 * (high - low)
    sigma = center / spread
    rho = 1.0 / sigma
    zero = jnp.zeros_like(center)
    e = [zero + 1.0, zero, zero, zero]
    d = [1.0 / center, zero, zero, zero]
    total = list(d)
    for _ in range(3):
        e = [e[0]] + [e[i] - d[i - 1] for i in range(1, 4)]
        rho_next = 1.0 / (2.0 * sigma - rho)
        d = [rho_next * rho * d[i] + (2.0 * rho_next / spread) * e[i] for i in range(4)]
        total = [a + b for a, b in zip(total, d)]
        rho = rho_next
    total = [jnp.concatenate([c] * (cw // 128), axis=1) for c in total]

    pltpu.make_async_copy(zrecv, zrecv, z_sem.at[0]).wait()
    for k in range(n_gy):
        x = warm[:, cw * k : cw * k + cw]
        for j in range(4):
            x = x + total[j] * zrecv[k, j]
        o_warm[:, cw * k : cw * k + cw] = x

    for copy in second:
        copy.wait_send()
    for cond, copy in sends:
        sent_if(cond, copy)
    part = pl.ds(0, n_gy - 1)
    remote(tsend.at[part], trecv.at[part], t_sem.at[1], t_sem.at[0], (gx, right)).wait_send()
    sent_if(has_u, far_u)
    sent_if(has_d, far_d)
    remote(
        asend.at[pl.ds(0, n_gy - 1)], arecv.at[pl.ds(0, n_gy - 1)], a_sem.at[1], a_sem.at[0],
        (gx, right),
    ).wait_send()
    for copy in coarse_rows:
        copy.wait_send()
    part = pl.ds(0, n_gy - 1)
    remote(zsend.at[part], zrecv.at[part], z_sem.at[1], z_sem.at[0], (gx, right)).wait_send()
    remote(mrecv, mrecv, m_sem.at[1], m_sem.at[0], (gx, right)).wait_send()


def put_out(su, speed, dam, warm, o_shift, o_speed, o_dam, o_warm, sem):
    nt = dam.shape[1]
    hh = dam.shape[2]
    out = [pltpu.make_async_copy(warm, o_warm, sem.at[3 * nt])]
    for t in range(nt):
        cols = slice(128 * t, 128 * t + 128)
        out += [
            pltpu.make_async_copy(
                su.at[:, t, HALO : HALO + hh, :], o_shift.at[:, :, cols], sem.at[3 * t]
            ),
            pltpu.make_async_copy(speed.at[:, t], o_speed.at[:, :, cols], sem.at[3 * t + 1]),
            pltpu.make_async_copy(dam.at[:, t], o_dam.at[:, :, cols], sem.at[3 * t + 2]),
        ]
    for copy in out:
        copy.start()
    for copy in out:
        copy.wait()


def per_device(n_gx, n_gy, shift, speed, level, mark, warm, store, film, bath):
    _, hh, ww = shift.shape
    rpd, _ = warm.shape
    cw, ch = ww // 2, hh // 2
    wide = cw + 128
    nt, nct = ww // 128, cw // 128
    ntile = nt + 1
    crows, frows = ch + 16, hh + 2 * HALO
    nsl = n_gy + 2 * (HALO // rpd)
    vm = lambda *s: pltpu.VMEM(s, F32)
    dma = lambda n: pltpu.SemaphoreType.DMA((n,))
    hbm = pl.BlockSpec(memory_space=pltpu.HBM)
    vmem = pl.BlockSpec(memory_space=pltpu.VMEM)
    outs = pl.pallas_call(
        functools.partial(kernel, n_gx, n_gy),
        out_shape=(
            vm(2, ntile, frows, 128),
            vm(2, nt, hh, 128),
            pltpu.VMEM((2, nt, hh, 128), jnp.bfloat16),
            vm(*warm.shape),
        ),
        in_specs=[hbm] * 8,
        out_specs=(vmem,) * 4,
        scratch_shapes=[
            vm(n_gy, rpd, wide),
            vm(nsl, rpd, wide),
            vm(n_gy, 2, rpd, wide),
            vm(n_gy, 2, rpd, wide),
            vm(2, hh, 128),
            vm(2, hh, 128),
            vm(4, 8, 128),
            vm(2, 6 * nt + 1, 8, 128),
            vm(2, 6 * nt + 1, 8, 128),
            vm(2, 6, ntile, 8, 128),
            vm(SUBSTEPS + 1, 2, ntile, 8, 128),
            vm(SUBSTEPS, 2, ntile, 8, 128),
            pltpu.VMEM(level.shape, level.dtype),
            vm(*warm.shape),
            vm(*warm.shape),
            vm(*warm.shape),
            vm(*warm.shape),
            vm(2, ntile, frows, 128),
            vm(2, ntile, frows, 128),
            vm(frows, 128),
            vm(frows, 128),
            vm(ntile, frows, 128),
            vm(ntile, frows, 128),
            vm(ntile, frows, 128),
            vm(2, ntile, frows + 8, 128),
            vm(nct + 1, crows, 128),
            vm(2, crows, wide),
            vm(nct + 1, frows, 128),
            vm(256, 128),
            vm(nt, hh, 128),
            vm(ch, cw),
            vm(2, 8, cw),
            vm(crows, 128),
            vm(crows, 128),
            vm(n_gy, 4, rpd, cw),
            vm(n_gy, 4, rpd, cw),
            vm(1, 128),
            vm(n_gx * n_gy - 1, 1, 128),
            dma(8),
            dma(8),
            dma(4),
            dma(2),
            dma(6),
            dma(8),
            dma(8),
            dma(2),
            dma(2),
            dma(8),
            pltpu.SMEM((1, hh // SR), mark.dtype),
        ],
        compiler_params=pltpu.CompilerParams(
            collective_id=0, has_side_effects=True
        ),
    )(shift, speed, level, mark.reshape(1, hh // SR), warm, store, film, bath)
    return pl.pallas_call(
        put_out,
        out_shape=tuple(
            jax.ShapeDtypeStruct(o.shape, d)
            for o, d in ((shift, F32), (speed, F32), (level, jnp.bfloat16), (warm, F32))
        ),
        in_specs=[vmem] * 4,
        out_specs=(hbm,) * 4,
        scratch_shapes=[dma(3 * nt + 1)],
    )(*(pltpu.with_memory_space_constraint(o, pltpu.VMEM) for o in outs))


def solution(mesh):
    rows = P(("gx", "gy"), None)
    plate = P(None, "gx", "gy")
    return jax.shard_map(
        functools.partial(per_device, mesh.shape["gx"], mesh.shape["gy"]),
        mesh=mesh,
        in_specs=(plate, plate, plate, P("gx", "gy"), rows, rows, rows, rows),
        out_specs=(plate, plate, plate, rows),
        check_vma=False,
    )
```

time: 30.1 us -> 27.5 us (0.914)
  Pallas kernels: 29.2 us -> 26.7 us
    pallas_call x2, Pallas kernels: 29.2 us -> 26.7 us  [the longest x1 25.7 us: per_device(): pl.pallas_call(functools.partial(kernel, n_gx, n_gy), out_shape=(vm(2, nt...]
where the time goes in v2:
time: 27.5 us; the launch traced here: 27.3 us
  Pallas kernels  26.7 us (97%)
  between operations  0.64 us (2%)
    pallas_call x1, Pallas kernels, per_device(): pl.pallas_call(functools.partial(kernel, n_gx, n_gy), out_shape=(vm(2, nt...  25.7 us
    pallas_call x1, Pallas kernels, per_device(): pl.pallas_call(put_out, out_shape=tuple((jax.ShapeDtypeStruct(o.shape, d)...  0.94 us

profile of v2, /device:TPU:0, one launch (start us, length us, event | category | flops | bytes accessed | tf_op | source)
XLA Modules:
  0.0 27.3 jit_solution(9697475541507713631)
XLA Ops:
  0.6 25.7 %shard_map.111 = (f32[2,5,80,128]{3,2,1,0:T(8,128)S(1)}, f32[2,4,64,128]{3,2,1,0:T(8,128)S(1)}, bf16[2,4,64,128]{3,2,1,0:T(8,128)(2,1)S(1)}, f32[4,2048]{1,0:T(4,128)S(1)}) custom-call(f32[2,64,512]{2,1,0:T(8,128)} %shift.1, f32[2,64,512]{2,1,0:T(8,128)} %speed.1, s32[2,64,512]{2,1,0:T(8,128)} %level_h.1, s32[1,8]{1,0:T(1,128)} %bitcast.1, ...), custom_call_target="tpu_custom_call" | custom-call | tf_op jit(solution)/shard_map/pallas_call | solution.py:734
  26.4 0.9 %shard_map.112 = (f32[2,64,512]{2,1,0:T(8,128)}, f32[2,64,512]{2,1,0:T(8,128)}, bf16[2,64,512]{2,1,0:T(8,128)(2,1)}, f32[4,2048]{1,0:T(4,128)}) custom-call(f32[2,5,80,128]{3,2,1,0:T(8,128)S(1)} %get-tuple-element.8.su, f32[2,4,64,128]{3,2,1,0:T(8,128)S(1)} %get-tuple-element.9.speed, bf16[2,4,64,128]{3,2,1,0:T(8,128)(2,1)S(1)} %get-tuple-element.10.dam, ...), custom_call_target="tpu_custom_call" | custom-call | tf_op jit(solution)/shard_map/pallas_call | solution.py:799

commit v3 on v2

--- a/solution.py
+++ b/solution.py
@@ -74,28 +74,25 @@
     fine,
     nx,
     tcx,
-    acf,
     widebuf,
     tab_s,
     gap,
-    cbuf,
-    crow,
-    ccl,
-    ccr,
-    zsend,
-    zrecv,
+    base_t,
+    cpad,
+    erow,
+    grow_c,
+    ecol,
+    gcol_c,
+    cb4,
+    owc,
+    own3,
+    field,
+    zown,
     msend,
     mrecv,
-    n_send,
-    n_recv,
-    t_sem,
-    far_sem,
-    a_sem,
-    c_send,
-    c_recv,
-    z_sem,
-    m_sem,
-    in_sem,
+    s_sem,
+    r_sem,
+    meter,
     mark,
 ):
     ndev = n_gx * n_gy
@@ -119,10 +116,29 @@
     right = lax.rem(gy + 1, n_gy)
     has_u, has_d = gx > 0, gx < n_gx - 1
     has_l, has_r = gy > 0, gy < n_gy - 1
+    hz = HALO // 2 // rpd
+    span = cw * n_gy
     own_r = slice(HALO, HALO + hh)
 
+    n_v = jnp.where(has_u, 1, 0) + jnp.where(has_d, 1, 0)
+    n_h = jnp.where(has_l, 1, 0) + jnp.where(has_r, 1, 0)
+
+    def size(ref):
+        return math.prod(ref.shape) // 128
+
+    def done(sem, lines):
+        part = meter.at[pl.ds(0, lines)]
+        pltpu.make_async_copy(part, part, sem).wait()
+
+    def done_if(cond, sem, lines):
+        if lines:
+
+            @pl.when(cond)
+            def _():
+                done(sem, lines)
+
     barrier = pltpu.get_barrier_semaphore()
-    warm_load = pltpu.make_async_copy(warm_h, warm, in_sem.at[0])
+    warm_load = pltpu.make_async_copy(warm_h, warm, r_sem.at[9])
     warm_load.start()
 
     def greet(a, b):
@@ -137,31 +153,24 @@
             greet(a, b)
 
     loads = [
-        pltpu.make_async_copy(src, dst, in_sem.at[i])
-        for i, (src, dst) in enumerate(
-            (
-                (mark_h, mark),
-                (level_h, level),
-                (store_h, store),
-                (film_h, film),
-                (bath_h, bath),
-            ),
-            1,
+        pltpu.make_async_copy(src, dst, r_sem.at[i])
+        for src, dst, i in (
+            (mark_h, mark, 1),
+            (level_h, level, 10),
+            (store_h, store, 11),
+            (film_h, film, 11),
+            (bath_h, bath, 11),
         )
     ]
     loads[0].start()
     loads[1].start()
-    for src, dst, i in ((shift, su, 6), (speed, sv, 7)):
+    for src, dst in ((shift, su), (speed, sv)):
         for t in range(nt):
             pltpu.make_async_copy(
-                src.at[:, :, 128 * t : 128 * t + 128], dst.at[:, t, own_r, :], in_sem.at[i]
+                src.at[:, :, 128 * t : 128 * t + 128], dst.at[:, t, own_r, :], r_sem.at[10]
             ).start()
     for copy in loads[2:]:
         copy.start()
-
-    def loaded(dst, i):
-        part = dst.at[:, 0:nt, own_r, :]
-        pltpu.make_async_copy(part, part, in_sem.at[i]).wait()
 
     lane_c = lane_iota((rpd, 128))
 
@@ -185,31 +194,26 @@
 
     pl.semaphore_wait(barrier, n_gy + n_gx + 2)
 
-    def along(k, c):
+    for k in range(1, n_gy):
         t = lax.rem(gy + k, n_gy)
-        remote(tsend.at[t], trecv.at[gy + hb], t_sem.at[1], t_sem.at[0], (gx, t)).start()
-        return c
-
-    lax.fori_loop(1, n_gy, along, 0)
-    pltpu.make_async_copy(tsend.at[gy], trecv.at[gy + hb], t_sem.at[0]).start()
+        remote(tsend.at[t], trecv.at[gy + hb], s_sem.at[0], r_sem.at[3], (gx, t)).start()
+    pltpu.make_async_copy(tsend.at[gy], trecv.at[gy + hb], r_sem.at[3]).start()
 
     sharp = -4.0 * math.log2(math.e)
     lane = lane_iota((hh, 128))
     loads[0].wait()
+    done(r_sem.at[10], 3 * size(level))
     for s in range(hh // SR):
         kw[HALO + SR * s : HALO + SR * s + SR, :] = (
             jnp.full((SR, 128), mark[0, s], jnp.int32).astype(F32) * sharp
         )
     w_own = kw[own_r, :] * (0.125 / sharp)
     grow = gx * hh + row_iota((hh, 128))
-    loads[1].wait()
     for t in range(nt):
         cols = slice(128 * t, 128 * t + 128)
         gcol = gy * ww + 128 * t + lane
         ss[0, t, own_r, :] = jnp.where(grow >= 1, 1.0 - level[0, :, cols].astype(F32) * w_own, 0.0)
         ss[1, t, own_r, :] = jnp.where(gcol >= 1, 1.0 - level[1, :, cols].astype(F32) * w_own, 0.0)
-    loaded(su, 6)
-    loaded(sv, 7)
     for c in range(2):
         for t in range(nt):
             sv[c, t, own_r, :] = 0.4 * sv[c, t, own_r, :]
@@ -228,17 +232,17 @@
         acc_r = jnp.where(here, pltpu.roll(last, 8 * f + 8, 1), acc_r)
     pk[0] = acc_l
     pk[1] = acc_r
-    side_l = remote(pk.at[0], rk.at[1], n_send.at[0], n_recv.at[1], (gx, left))
-    side_r = remote(pk.at[1], rk.at[0], n_send.at[1], n_recv.at[0], (gx, right))
+    side_l = remote(pk.at[0], rk.at[1], s_sem.at[3], r_sem.at[0], (gx, left))
+    side_r = remote(pk.at[1], rk.at[0], s_sem.at[4], r_sem.at[0], (gx, right))
     top, end = slice(0, 8), slice(hh - 8, hh)
     corners = [
-        (has_u & has_l, remote(pk.at[0, top], ck.at[3], n_send.at[2], n_recv.at[5], (up, left)), 2),
-        (has_u & has_r, remote(pk.at[1, top], ck.at[2], n_send.at[3], n_recv.at[4], (up, right)), 3),
-        (has_d & has_l, remote(pk.at[0, end], ck.at[1], n_send.at[4], n_recv.at[3], (down, left)), 4),
-        (has_d & has_r, remote(pk.at[1, end], ck.at[0], n_send.at[5], n_recv.at[2], (down, right)), 5),
+        (has_u & has_l, remote(pk.at[0, top], ck.at[3], s_sem.at[1], r_sem.at[2], (up, left)), 2),
+        (has_u & has_r, remote(pk.at[1, top], ck.at[2], s_sem.at[1], r_sem.at[2], (up, right)), 3),
+        (has_d & has_l, remote(pk.at[0, end], ck.at[1], s_sem.at[2], r_sem.at[2], (down, left)), 4),
+        (has_d & has_r, remote(pk.at[1, end], ck.at[0], s_sem.at[2], r_sem.at[2], (down, right)), 5),
     ]
-    rows_u = remote(rowsend.at[0], rowrecv.at[1], n_send.at[6], n_recv.at[7], (up, gy))
-    rows_d = remote(rowsend.at[1], rowrecv.at[0], n_send.at[7], n_recv.at[6], (down, gy))
+    rows_u = remote(rowsend.at[0], rowrecv.at[1], s_sem.at[1], r_sem.at[2], (up, gy))
+    rows_d = remote(rowsend.at[1], rowrecv.at[0], s_sem.at[2], r_sem.at[2], (down, gy))
     sends = [(has_l, side_l), (has_r, side_r)] + [(a, b) for a, b, _ in corners]
     sends += [(has_u, rows_u), (has_d, rows_d)]
 
@@ -251,11 +255,6 @@
         @pl.when(cond)
         def _():
             copy.wait_send()
-
-    def came_if(cond, copy):
-        @pl.when(cond)
-        def _():
-            copy.wait_recv()
 
     for cond, copy in sends[0:6]:
         start_if(cond, copy)
@@ -272,15 +271,13 @@
     col = (2 * (n_i % 64)).astype(F32)
     tab = jnp.exp(jnp.abs(pos - col) * (-4.0 / SEG)) + jnp.exp(jnp.abs(pos - col - 1.0) * (-4.0 / SEG))
     tab_s[...] = jnp.where(k_i // SEG == n_i // 64, tab * (1.0 / SEG), 0.0)
-    for i in (2, 3, 4):
-        loads[i].wait()
+    done(r_sem.at[11], 3 * size(store))
     base = store[...] + film[...]
-    force_own = store[...] * t_own + film[...] * bath[...]
+    own3[0, hz] = t_own
+    own3[1, hz] = base
+    own3[2, hz] = store[...] * t_own + film[...] * bath[...]
     for k in range(n_gy):
-        for q, val in enumerate((base, force_own)):
-            main, edge = chunk(val, k)
-            asend[k, q, :, 0:cw] = main
-            asend[k, q, :, cw : cw + 128] = edge
+        asend[k] = base[:, cw * k : cw * k + cw]
     for strip in ((nstrip - 2) * 8, nstrip * 8):
         nx[:, :, strip : strip + 8, :] = jnp.zeros((2, ntile, 8, 128), F32)
     keeps = (slice(16, 24), slice(frows - 24, frows - 16))
@@ -290,25 +287,36 @@
                 keep[i, f, t] = ref[c, t, rows, :]
 
     mid = trecv.at[pl.ds(hb, n_gy)]
-    pltpu.make_async_copy(mid, mid, t_sem.at[0]).wait()
+    pltpu.make_async_copy(mid, mid, r_sem.at[3]).wait()
     far_u = remote(
-        trecv.at[pl.ds(hb, hb)], trecv.at[pl.ds(hb + n_gy, hb)], t_sem.at[2], far_sem.at[1], (up, gy)
+        trecv.at[pl.ds(hb, hb)], trecv.at[pl.ds(hb + n_gy, hb)], s_sem.at[1], r_sem.at[2], (up, gy)
     )
     far_d = remote(
-        trecv.at[pl.ds(n_gy, hb)], trecv.at[pl.ds(0, hb)], t_sem.at[3], far_sem.at[0], (down, gy)
+        trecv.at[pl.ds(n_gy, hb)], trecv.at[pl.ds(0, hb)], s_sem.at[2], r_sem.at[2], (down, gy)
     )
     start_if(has_u, far_u)
     start_if(has_d, far_d)
 
     def late(k, c):
         t = lax.rem(gy + k, n_gy)
-        remote(asend.at[t], arecv.at[gy], a_sem.at[1], a_sem.at[0], (gx, t)).start()
+        remote(asend.at[t], arecv.at[gy], s_sem.at[0], r_sem.at[4], (gx, t)).start()
         return c
 
     lax.fori_loop(1, n_gy, late, 0)
-    pltpu.make_async_copy(asend.at[gy], arecv.at[gy], a_sem.at[0]).start()
-    crows = ch + 16
-    wide = cw + 128
+    pltpu.make_async_copy(asend.at[gy], arecv.at[gy], r_sem.at[4]).start()
+    mine = own3.at[:, hz]
+    swaps = []
+    for d in range(1, hz + 1):
+        for i, to, ok, came in (
+            (d - 1, me + d, me + d < ndev, me >= d),
+            (hz + d - 1, me - d, me >= d, me + d < ndev),
+        ):
+            at = hz - d if i < hz else hz + d
+            to = lax.rem(to + ndev, ndev)
+            copy = remote(mine, own3.at[:, at], s_sem.at[5 + i], r_sem.at[5], (to // n_gy, to % n_gy))
+            swaps.append((ok, came, copy))
+    for ok, _, copy in swaps:
+        start_if(ok, copy)
     lane8 = lane_iota((8, 128))
     first_lane, last_lane = lane8 == 0, lane8 == 127
 
@@ -382,8 +390,8 @@
     for s in range(2, nstrip - 2):
         heat_x(s)
 
-    came_if(has_l, side_r)
-    came_if(has_r, side_l)
+    for h in (1, 2):
+        done_if(n_h == h, r_sem.at[0], h * size(pk.at[0]))
 
     def unpack(got_l, got_r, rows, outside):
         shape = got_l.shape
@@ -460,10 +468,17 @@
 
     lax.fori_loop(0, SUBSTEPS, interior, 0)
 
+    far_size = hb * size(trecv.at[0])
+    for v in (1, 2):
+        for h in (1, 2):
+            done_if(
+                (n_v == v) & (n_h == h),
+                r_sem.at[2],
+                v * (size(rowsend.at[0]) + far_size + h * size(ck.at[0])),
+            )
     for side, (here, at, slot, line) in enumerate(
         ((has_u, 0, 0, 8), (has_d, ch + 8, hb + n_gy, ch + 7))
     ):
-        came_if(here, far_u if side else far_d)
 
         @pl.when(here)
         def _():
@@ -484,12 +499,6 @@
     for s in (0, 1, 2, nstrip - 2, nstrip - 1):
         heat_x(s)
 
-    came_if(has_u & has_l, corners[3][1])
-    came_if(has_u & has_r, corners[2][1])
-    came_if(has_d & has_l, corners[1][1])
-    came_if(has_d & has_r, corners[0][1])
-    came_if(has_u, rows_d)
-    came_if(has_d, rows_u)
     for side, (here, at) in enumerate(((has_u, 0), (has_d, hh + HALO))):
         rows = slice(at, at + 8)
         for f, (ref, c) in enumerate(fields):
@@ -526,19 +535,6 @@
     for c in range(2):
         for t in range(ntile):
             su[c, t, line : line + 1, :] = hist_n[SUBSTEPS, c, t, 0:1, :]
-
-    pltpu.make_async_copy(arecv, arecv, a_sem.at[0]).wait()
-    for k in range(n_gy):
-        for q in range(2):
-            acf[q, 8 + rpd * k : 8 + rpd * k + rpd, :] = arecv[k, q]
-    coarse_rows = [
-        remote(
-            acf.at[:, 8:16], acf.at[:, ch + 8 : ch + 16], a_sem.at[2], a_sem.at[4], (up, gy)
-        ),
-        remote(acf.at[:, ch : ch + 8], acf.at[:, 0:8], a_sem.at[3], a_sem.at[5], (down, gy)),
-    ]
-    for copy in coarse_rows:
-        copy.start()
 
     for t in range(nt):
         gcol = gy * ww + 128 * t + lane
@@ -559,102 +555,171 @@
         jnp.concatenate([rows2[:, 256 * t : 256 * t + 256] for t in range(pairs)], axis=0), tab_s[...]
     )
     resist = jnp.concatenate([glow[ch * t : ch * t + ch] for t in range(pairs)], axis=1)
-    t_all = jnp.concatenate([tcx[j] for j in range(nct + 1)], axis=1)
-    cond_own = (1.0 + 0.5 * t_all[8 : 8 + ch, 0:cw]) / (1.0 + resist)
-    cbuf[...] = cond_own
-    def neighbours(send_l, send_r, row_u, row_d, recv_l, recv_r, got_u, got_d, rows, ssem, rsem):
-        top, end = slice(0, 8), slice(rows - 8, rows)
-        lo, mid, hi = slice(0, 8), slice(8, rows + 8), slice(rows + 8, rows + 16)
-        return [
-            remote(row_u, got_d, ssem.at[0], rsem.at[0], (up, gy)),
-            remote(row_d, got_u, ssem.at[1], rsem.at[1], (down, gy)),
-            remote(send_l, recv_r.at[mid], ssem.at[2], rsem.at[2], (gx, left)),
-            remote(send_r, recv_l.at[mid], ssem.at[3], rsem.at[3], (gx, right)),
-            remote(send_l.at[top], recv_r.at[hi], ssem.at[4], rsem.at[4], (up, left)),
-            remote(send_r.at[top], recv_l.at[hi], ssem.at[5], rsem.at[5], (up, right)),
-            remote(send_l.at[end], recv_r.at[lo], ssem.at[6], rsem.at[6], (down, left)),
-            remote(send_r.at[end], recv_l.at[lo], ssem.at[7], rsem.at[7], (down, right)),
-        ]
-
-    second = neighbours(
-        cbuf.at[:, 0:128], cbuf.at[:, cw - 128 : cw], cbuf.at[0:8], cbuf.at[ch - 8 : ch],
-        ccl, ccr, crow.at[0], crow.at[1], ch, c_send, c_recv,
-    )
-    for copy in second:
-        copy.start()
+    t_tile = jnp.concatenate([tcx[j, 8 : 8 + ch, :] for j in range(nct)], axis=1)
+    cond = (1.0 + 0.5 * t_tile) / (1.0 + resist)
+    for j in range(nct):
+        cpad[j, 8 : 8 + ch, :] = cond[:, 128 * j : 128 * j + 128]
+    erow[0] = cond[0:1, :]
+    erow[1] = cond[ch - 1 : ch, :]
+    first_col, last_col = cond[0:8, 0:128], pltpu.roll(cond[0:8, cw - 128 : cw], 1, 1)
+    for i in range(1, ch // 8):
+        rows = slice(8 * i, 8 * i + 8)
+        here = lane8 == i
+        first_col = jnp.where(here, pltpu.roll(cond[rows, 0:128], i, 1), first_col)
+        last_col = jnp.where(here, pltpu.roll(cond[rows, cw - 128 : cw], i + 1, 1), last_col)
+    ecol[0] = first_col
+    ecol[1] = last_col
+    beside = [
+        (has_u, has_d, remote(erow.at[0], grow_c.at[1], s_sem.at[1], r_sem.at[6], (up, gy))),
+        (has_d, has_u, remote(erow.at[1], grow_c.at[0], s_sem.at[2], r_sem.at[6], (down, gy))),
+        (has_l, has_r, remote(ecol.at[0], gcol_c.at[1], s_sem.at[3], r_sem.at[6], (gx, left))),
+        (has_r, has_l, remote(ecol.at[1], gcol_c.at[0], s_sem.at[4], r_sem.at[6], (gx, right))),
+    ]
+    for ok, _, copy in beside:
+        start_if(ok, copy)
+    for b in range(n_gy):
+        cb4[b] = cond[rpd * b : rpd * b + rpd, :]
+    my_cols = pl.ds(pl.multiple_of(gy * cw, 128), cw)
+    to_owner = []
+    for t in range(n_gy):
+        lo, hi = max(0, t - hz), min(n_gy, t + hz + 1)
+        src = cb4.at[pl.ds(lo, hi - lo)]
+        dst = owc.at[pl.ds(lo - t + hz, hi - lo), :, my_cols]
+        to_owner.append((gy != t, remote(src, dst, s_sem.at[0], r_sem.at[7], (gx, t))))
+        here = pltpu.make_async_copy(src, dst, r_sem.at[7])
+
+        @pl.when(gy == t)
+        def _():
+            here.start()
+
+    for t in range(hz):
+        n = hz - t
+        src, dst = cb4.at[pl.ds(n_gy - n, n)], owc.at[pl.ds(0, n), :, my_cols]
+        to_owner.append((has_d, remote(src, dst, s_sem.at[2], r_sem.at[7], (down, t))))
+        src, dst = cb4.at[pl.ds(0, n)], owc.at[pl.ds(2 * hz + 1 - n, n), :, my_cols]
+        to_owner.append((has_u, remote(src, dst, s_sem.at[1], r_sem.at[7], (up, n_gy - 1 - t))))
+    for ok, copy in to_owner:
+        start_if(ok, copy)
 
     for c in range(2):
         for t in range(nt):
             o_speed[c, t] = 2.5 * sv[c, t, own_r, :]
 
-    for copy in coarse_rows:
-        copy.wait_recv()
-
-    for copy in second:
-        copy.wait_recv()
-    lane_k = lane_iota((crows, 128))
-    cond = jnp.concatenate(
-        [
-            jnp.concatenate([crow[0], cbuf[...], crow[1]], axis=0),
-            jnp.where(lane_k < 64, ccr[...], ccl[...]),
-        ],
-        axis=1,
-    )
-    crow_i, clane_i = row_iota((crows, wide)), lane_iota((crows, wide))
-    crow_g = gx * ch - 8 + crow_i
-    ccol_g = gy * cw + jnp.where(clane_i < cw + 64, clane_i, clane_i - wide)
+    pltpu.make_async_copy(arecv, arecv, r_sem.at[4]).wait()
+    for k in range(n_gy):
+        for j in range(nct):
+            base_t[j, rpd * k : rpd * k + rpd, :] = arecv[k, :, 128 * j : 128 * j + 128]
+    for v in (1, 2):
+        for h in (1, 2):
+            done_if(
+                (n_v == v) & (n_h == h),
+                r_sem.at[6],
+                v * size(erow.at[0]) + h * size(ecol.at[0]),
+            )
+    for j in range(nct):
+        cols = slice(128 * j, 128 * j + 128)
+        cpad[j, 7:8, :] = jnp.where(has_u, grow_c[0, :, cols], 0.0)
+        cpad[j, 8 + ch : 9 + ch, :] = jnp.where(has_d, grow_c[1, :, cols], 0.0)
+    from_l, from_r = gcol_c[0], gcol_c[1]
+    sub8 = row_iota((8, 128))
+    peak = None
+    for i in range(ch // 8):
+        r0 = 8 + 8 * i
+        mid = [cpad[j, r0 : r0 + 8, :] for j in range(nct)]
+        fwd = [pltpu.roll(x, 1, 1) for x in mid]
+        bwd = [pltpu.roll(x, 127, 1) for x in mid]
+        fwd_in = [pltpu.roll(from_l, 128 - i, 1) if i else from_l] + fwd[:-1]
+        bwd_in = bwd[1:] + [pltpu.roll(from_r, 127 - i, 1)]
+        for j in range(nct):
+            c = mid[j]
+            f_u = c + cpad[j, r0 - 1 : r0 + 7, :]
+            f_d = c + cpad[j, r0 + 1 : r0 + 9, :]
+            f_l = c + jnp.where(first_lane, fwd_in[j], fwd[j])
+            f_r = c + jnp.where(last_lane, bwd_in[j], bwd[j])
+            if i == 0:
+                f_u = jnp.where(~has_u & (sub8 == 0), 0.0, f_u)
+            if i == ch // 8 - 1:
+                f_d = jnp.where(~has_d & (sub8 == 7), 0.0, f_d)
+            if j == 0:
+                f_l = jnp.where(~has_l & first_lane, 0.0, f_l)
+            if j == nct - 1:
+                f_r = jnp.where(~has_r & last_lane, 0.0, f_r)
+            off = 0.5 * ((f_u + f_d) + (f_l + f_r))
+            ratio = off / (base_t[j, 8 * i : 8 * i + 8, :] + off)
+            peak = ratio if peak is None else jnp.maximum(peak, ratio)
+    msend[...] = jnp.full((1, 128), jnp.max(peak), F32)
+
+    for k in range(1, ndev):
+        t = lax.rem(me + k, ndev)
+        remote(
+            msend, mrecv.at[k - 1], s_sem.at[0], r_sem.at[8], (t // n_gy, t % n_gy)
+        ).start()
+
+    orows = 16
+    n_swap = sum(jnp.where(came, 1, 0) for _, came, _ in swaps)
+    for n in range(1, 2 * hz + 1):
+        done_if(n_swap == n, r_sem.at[5], n * size(mine))
+    reach = hz * rpd
+
+    def gather(q, ref, fill):
+        for b in range(2 * hz + 1):
+            value = ref[b]
+            if b != hz:
+                there = me >= hz - b if b < hz else me + (b - hz) < ndev
+                value = jnp.where(there, value, fill)
+            field[q, rpd * b : rpd * b + rpd, :] = value
+
+    for q in range(3):
+        gather(q, own3.at[q], 1.0)
+    rest = (2 * hz + 1) * rpd
+    for q in range(4):
+        field[q, rest:orows, :] = jnp.full((orows - rest, span), 0.0 if q == 3 else 1.0, F32)
+
+    short_t = jnp.where(gx == 0, jnp.maximum(hz - gy, 0), 0)
+    short_b = jnp.where(gx == n_gx - 1, jnp.maximum(hz - (n_gy - 1 - gy), 0), 0)
+    for a in range(hz + 1):
+        for b in range(hz + 1):
+            got = owc.at[pl.ds(a, 2 * hz + 1 - a - b)]
+
+            @pl.when((short_t == a) & (short_b == b))
+            def _():
+                pltpu.make_async_copy(got, got, r_sem.at[7]).wait()
+
+    gather(3, owc, 0.0)
+    oshape = (orows, span)
+    row_g = me * rpd - reach + row_iota(oshape)
+    col_g = lane_iota(oshape)
+    total_rows = ndev * rpd
 
     def four(x):
         return (
             pltpu.roll(x, 1, 0),
-            pltpu.roll(x, crows - 1, 0),
+            pltpu.roll(x, orows - 1, 0),
             pltpu.roll(x, 1, 1),
-            pltpu.roll(x, wide - 1, 1),
+            pltpu.roll(x, span - 1, 1),
         )
 
+    inside = (row_g >= 0) & (row_g < total_rows)
     masks = (
-        crow_g >= 1,
-        crow_g <= ch * n_gx - 2,
-        ccol_g >= 1,
-        ccol_g <= cw * n_gy - 2,
+        inside & (row_g >= 1),
+        inside & (row_g <= total_rows - 2),
+        col_g >= 1,
+        col_g <= span - 2,
     )
-    faces = [
-        jnp.where(m, 0.5 * (cond + nb), 0.0) for m, nb in zip(masks, four(cond))
-    ]
-    offsum = faces[0] + faces[1] + faces[2] + faces[3]
-    diagonal = acf[0] + offsum
+    cond = field[3]
+    faces = [jnp.where(m, 0.5 * (cond + nb), 0.0) for m, nb in zip(masks, four(cond))]
+    diagonal = field[1] + (faces[0] + faces[1] + faces[2] + faces[3])
     inv = 1.0 / diagonal
-    ratio = offsum * inv
-    peak = jnp.max(ratio[8 : 8 + ch, 0:cw])
-    msend[...] = jnp.full((1, 128), peak, F32)
-
-    def tell(k, c):
-        t = lax.rem(me + k, ndev)
-        remote(
-            msend, mrecv.at[k - 1], m_sem.at[1], m_sem.at[0], (t // n_gy, t % n_gy)
-        ).start()
-        return c
-
-    lax.fori_loop(1, ndev, tell, 0)
-
+    t_all = field[0]
     near = sum(f * nb for f, nb in zip(faces, four(t_all)))
-    z = (acf[1] - (diagonal * t_all - near)) * inv
+    z = (field[2] - (diagonal * t_all - near)) * inv
     faces = [f * inv for f in faces]
     for j in range(4):
         if j:
             z = z - sum(f * nb for f, nb in zip(faces, four(z)))
-        for k in range(n_gy):
-            zsend[k, j] = z[8 + rpd * k : 8 + rpd * k + rpd, 0:cw]
-
-    def home(k, c):
-        t = lax.rem(gy + k, n_gy)
-        remote(zsend.at[t], zrecv.at[gy], z_sem.at[1], z_sem.at[0], (gx, t)).start()
-        return c
-
-    lax.fori_loop(1, n_gy, home, 0)
-    pltpu.make_async_copy(zsend.at[gy], zrecv.at[gy], z_sem.at[0]).start()
-
-    pltpu.make_async_copy(mrecv, mrecv, m_sem.at[0]).wait()
+        zown[j] = z[reach : reach + rpd, :]
+
+    pltpu.make_async_copy(mrecv, mrecv, r_sem.at[8]).wait()
     peak = jnp.maximum(jnp.max(mrecv[...], axis=0), msend[...])[0:1, :]
     low, high = 1.0 - peak, 1.0 + peak
     center = 0.5 * (high + low)
@@ -671,51 +736,45 @@
         d = [rho_next * rho * d[i] + (2.0 * rho_next / spread) * e[i] for i in range(4)]
         total = [a + b for a, b in zip(total, d)]
         rho = rho_next
-    total = [jnp.concatenate([c] * (cw // 128), axis=1) for c in total]
-
-    pltpu.make_async_copy(zrecv, zrecv, z_sem.at[0]).wait()
-    for k in range(n_gy):
-        x = warm[:, cw * k : cw * k + cw]
+    for t in range(span // 128):
+        cols = slice(128 * t, 128 * t + 128)
+        x = warm[:, cols]
         for j in range(4):
-            x = x + total[j] * zrecv[k, j]
-        o_warm[:, cw * k : cw * k + cw] = x
-
-    for copy in second:
-        copy.wait_send()
-    for cond, copy in sends:
-        sent_if(cond, copy)
-    part = pl.ds(0, n_gy - 1)
-    remote(tsend.at[part], trecv.at[part], t_sem.at[1], t_sem.at[0], (gx, right)).wait_send()
-    sent_if(has_u, far_u)
-    sent_if(has_d, far_d)
-    remote(
-        asend.at[pl.ds(0, n_gy - 1)], arecv.at[pl.ds(0, n_gy - 1)], a_sem.at[1], a_sem.at[0],
-        (gx, right),
-    ).wait_send()
-    for copy in coarse_rows:
-        copy.wait_send()
-    part = pl.ds(0, n_gy - 1)
-    remote(zsend.at[part], zrecv.at[part], z_sem.at[1], z_sem.at[0], (gx, right)).wait_send()
-    remote(mrecv, mrecv, m_sem.at[1], m_sem.at[0], (gx, right)).wait_send()
+            x = x + total[j] * zown[j, :, cols]
+        o_warm[:, cols] = x
+
+    for ok, _, copy in swaps:
+        sent_if(ok, copy)
+    always = (n_gy - 1) * (size(tsend.at[0]) + size(asend.at[0])) + (ndev - 1)
+    blocks = [min(n_gy, t + hz + 1) - max(0, t - hz) for t in range(n_gy)]
+    one = size(cb4.at[0])
+    for t in range(n_gy):
+        done_if(gy == t, s_sem.at[0], always + one * (sum(blocks) - blocks[t]))
+    tall = size(rowsend.at[0]) + far_size + size(erow.at[0]) + one * (hz * (hz + 1) // 2)
+    for i, ok in ((1, has_u), (2, has_d)):
+        for h in (1, 2):
+            done_if(ok & (n_h == h), s_sem.at[i], tall + h * size(ck.at[0]))
+    for i, ok in ((3, has_l), (4, has_r)):
+        done_if(ok, s_sem.at[i], size(pk.at[0]) + size(ecol.at[0]))
 
 
 def put_out(su, speed, dam, warm, o_shift, o_speed, o_dam, o_warm, sem):
-    nt = dam.shape[1]
-    hh = dam.shape[2]
-    out = [pltpu.make_async_copy(warm, o_warm, sem.at[3 * nt])]
+    nt, hh = dam.shape[1:3]
     for t in range(nt):
         cols = slice(128 * t, 128 * t + 128)
-        out += [
-            pltpu.make_async_copy(
-                su.at[:, t, HALO : HALO + hh, :], o_shift.at[:, :, cols], sem.at[3 * t]
-            ),
-            pltpu.make_async_copy(speed.at[:, t], o_speed.at[:, :, cols], sem.at[3 * t + 1]),
-            pltpu.make_async_copy(dam.at[:, t], o_dam.at[:, :, cols], sem.at[3 * t + 2]),
-        ]
-    for copy in out:
-        copy.start()
-    for copy in out:
-        copy.wait()
+        for i, (src, dst) in enumerate(
+            (
+                (su.at[:, t, HALO : HALO + hh, :], o_shift.at[:, :, cols]),
+                (speed.at[:, t], o_speed.at[:, :, cols]),
+                (dam.at[:, t], o_dam.at[:, :, cols]),
+            )
+        ):
+            pltpu.make_async_copy(src, dst, sem.at[i]).start()
+    last = pltpu.make_async_copy(warm, o_warm, sem.at[3])
+    last.start()
+    for i, dst in enumerate((o_shift, o_speed, o_dam)):
+        pltpu.make_async_copy(dst, dst, sem.at[i]).wait()
+    last.wait()
 
 
 def per_device(n_gx, n_gy, shift, speed, level, mark, warm, store, film, bath):
@@ -727,6 +786,7 @@
     ntile = nt + 1
     crows, frows = ch + 16, hh + 2 * HALO
     nsl = n_gy + 2 * (HALO // rpd)
+    hz = HALO // 2 // rpd
     vm = lambda *s: pltpu.VMEM(s, F32)
     dma = lambda n: pltpu.SemaphoreType.DMA((n,))
     hbm = pl.BlockSpec(memory_space=pltpu.HBM)
@@ -744,8 +804,8 @@
         scratch_shapes=[
             vm(n_gy, rpd, wide),
             vm(nsl, rpd, wide),
-            vm(n_gy, 2, rpd, wide),
-            vm(n_gy, 2, rpd, wide),
+            vm(n_gy, rpd, cw),
+            vm(n_gy, rpd, cw),
             vm(2, hh, 128),
             vm(2, hh, 128),
             vm(4, 8, 128),
@@ -768,28 +828,25 @@
             vm(ntile, frows, 128),
             vm(2, ntile, frows + 8, 128),
             vm(nct + 1, crows, 128),
-            vm(2, crows, wide),
             vm(nct + 1, frows, 128),
             vm(256, 128),
             vm(nt, hh, 128),
-            vm(ch, cw),
-            vm(2, 8, cw),
-            vm(crows, 128),
-            vm(crows, 128),
-            vm(n_gy, 4, rpd, cw),
-            vm(n_gy, 4, rpd, cw),
+            vm(nct, ch, 128),
+            vm(nct, crows, 128),
+            vm(2, 1, cw),
+            vm(2, 1, cw),
+            vm(2, 8, 128),
+            vm(2, 8, 128),
+            vm(n_gy, rpd, cw),
+            vm(2 * hz + 1, rpd, cw * n_gy),
+            vm(3, 2 * hz + 1, rpd, cw * n_gy),
+            vm(4, 16, cw * n_gy),
+            vm(4, rpd, cw * n_gy),
             vm(1, 128),
             vm(n_gx * n_gy - 1, 1, 128),
-            dma(8),
-            dma(8),
-            dma(4),
-            dma(2),
-            dma(6),
-            dma(8),
-            dma(8),
-            dma(2),
-            dma(2),
-            dma(8),
+            dma(5 + 2 * hz),
+            dma(12),
+            vm(3 * level.size // 128, 1, 128),
             pltpu.SMEM((1, hh // SR), mark.dtype),
         ],
         compiler_params=pltpu.CompilerParams(
@@ -804,7 +861,7 @@
         ),
         in_specs=[vmem] * 4,
         out_specs=(hbm,) * 4,
-        scratch_shapes=[dma(3 * nt + 1)],
+        scratch_shapes=[dma(4)],
     )(*(pltpu.with_memory_space_constraint(o, pltpu.VMEM) for o in outs))
 
 

time: 27.5 us -> 25.1 us (0.913)
  Pallas kernels: 26.7 us -> 24.3 us
    pallas_call x1, Pallas kernels: 25.7 us -> 23.4 us  [per_device(): pl.pallas_call(functools.partial(kernel, n_gx, n_gy), out_shape=(vm(2, nt...]
where the time goes in v3:
time: 25.1 us; the launch traced here: 24.9 us
  Pallas kernels  24.3 us (97%)
  between operations  0.64 us (3%)
    pallas_call x1, Pallas kernels, per_device(): pl.pallas_call(functools.partial(kernel, n_gx, n_gy), out_shape=(vm(2, nt...  23.4 us
    pallas_call x1, Pallas kernels, per_device(): pl.pallas_call(put_out, out_shape=tuple((jax.ShapeDtypeStruct(o.shape, d)...  0.87 us

profile of v3, /device:TPU:0, one launch (start us, length us, event | category | flops | bytes accessed | tf_op | source)
XLA Modules:
  0.0 24.9 jit_solution(10945785340879773545)
XLA Ops:
  0.6 23.4 %shard_map.111 = (f32[2,5,80,128]{3,2,1,0:T(8,128)S(1)}, f32[2,4,64,128]{3,2,1,0:T(8,128)S(1)}, bf16[2,4,64,128]{3,2,1,0:T(8,128)(2,1)S(1)}, f32[4,2048]{1,0:T(4,128)S(1)}) custom-call(f32[2,64,512]{2,1,0:T(8,128)} %shift.1, f32[2,64,512]{2,1,0:T(8,128)} %speed.1, s32[2,64,512]{2,1,0:T(8,128)} %level_h.1, s32[1,8]{1,0:T(1,128)} %bitcast.1, ...), custom_call_target="tpu_custom_call" | custom-call | tf_op jit(solution)/shard_map/pallas_call | solution.py:794
  24.1 0.9 %shard_map.112 = (f32[2,64,512]{2,1,0:T(8,128)}, f32[2,64,512]{2,1,0:T(8,128)}, bf16[2,64,512]{2,1,0:T(8,128)(2,1)}, f32[4,2048]{1,0:T(4,128)}) custom-call(f32[2,5,80,128]{3,2,1,0:T(8,128)S(1)} %get-tuple-element.8.su, f32[2,4,64,128]{3,2,1,0:T(8,128)S(1)} %get-tuple-element.9.speed, bf16[2,4,64,128]{3,2,1,0:T(8,128)(2,1)S(1)} %get-tuple-element.10.dam, ...), custom_call_target="tpu_custom_call" | custom-call | tf_op jit(solution)/shard_map/pallas_call | solution.py:856

commit v4 on v3

--- a/solution.py
+++ b/solution.py
@@ -27,6 +27,20 @@
 
 def full_dot(a, b):
     return jnp.dot(a, b, precision=lax.Precision.HIGHEST, preferred_element_type=F32)
+
+
+def partner(me, k, n):
+    if n & (n - 1):
+        return lax.rem(me + k, n)
+    t = me
+    for b in range(n.bit_length() - 1):
+        if k >> b & 1:
+            t = t + (1 - 2 * (me // 2**b % 2)) * 2**b
+    return t
+
+
+def far_first(n, hops):
+    return sorted(range(1, n), key=lambda k: (-hops(k), -k))
 
 
 def pick(x, index):
@@ -57,9 +71,12 @@
     ck,
     rowsend,
     rowrecv,
-    keep,
-    hist_n,
-    hist_u,
+    bu,
+    bv,
+    bs,
+    bn,
+    past,
+    past_n,
     level,
     warm,
     store,
@@ -144,8 +161,8 @@
     def greet(a, b):
         pl.semaphore_signal(barrier, inc=1, device_id=(a, b), device_id_type=MESH)
 
-    for k in range(1, n_gy):
-        greet(gx, lax.rem(gy + k, n_gy))
+    for k in far_first(n_gy, lambda k: k // 2):
+        greet(gx, partner(gy, k, n_gy))
     for k in range(1, n_gx):
         greet(lax.rem(gx + k, n_gx), gy)
     for a in (up, down):
@@ -194,8 +211,8 @@
 
     pl.semaphore_wait(barrier, n_gy + n_gx + 2)
 
-    for k in range(1, n_gy):
-        t = lax.rem(gy + k, n_gy)
+    for k in far_first(n_gy, lambda k: k // 2):
+        t = partner(gy, k, n_gy)
         remote(tsend.at[t], trecv.at[gy + hb], s_sem.at[0], r_sem.at[3], (gx, t)).start()
     pltpu.make_async_copy(tsend.at[gy], trecv.at[gy + hb], r_sem.at[3]).start()
 
@@ -278,13 +295,9 @@
     own3[2, hz] = store[...] * t_own + film[...] * bath[...]
     for k in range(n_gy):
         asend[k] = base[:, cw * k : cw * k + cw]
-    for strip in ((nstrip - 2) * 8, nstrip * 8):
-        nx[:, :, strip : strip + 8, :] = jnp.zeros((2, ntile, 8, 128), F32)
-    keeps = (slice(16, 24), slice(frows - 24, frows - 16))
-    for i, rows in enumerate(keeps):
-        for f, (ref, c) in enumerate(fields):
-            for t in range(nt):
-                keep[i, f, t] = ref[c, t, rows, :]
+    strip = (nstrip - 2) * 8
+    nx[:, :, strip : strip + 8, :] = jnp.zeros((2, ntile, 8, 128), F32)
+    bn[:, :, :, 32:40, :] = jnp.zeros((2, 2, ntile, 8, 128), F32)
 
     mid = trecv.at[pl.ds(hb, n_gy)]
     pltpu.make_async_copy(mid, mid, r_sem.at[3]).wait()
@@ -297,12 +310,9 @@
     start_if(has_u, far_u)
     start_if(has_d, far_d)
 
-    def late(k, c):
-        t = lax.rem(gy + k, n_gy)
+    for k in range(1, n_gy):
+        t = partner(gy, k, n_gy)
         remote(asend.at[t], arecv.at[gy], s_sem.at[0], r_sem.at[4], (gx, t)).start()
-        return c
-
-    lax.fori_loop(1, n_gy, late, 0)
     pltpu.make_async_copy(asend.at[gy], arecv.at[gy], r_sem.at[4]).start()
     mine = own3.at[:, hz]
     swaps = []
@@ -393,7 +403,7 @@
     for h in (1, 2):
         done_if(n_h == h, r_sem.at[0], h * size(pk.at[0]))
 
-    def unpack(got_l, got_r, rows, outside):
+    def unpack(got_l, got_r, targets, rows, lines, outside):
         shape = got_l.shape
         lanes = lane_iota(shape)
         gone = outside | (~has_l & (lanes >= 64)) | (~has_r & (lanes < 64))
@@ -403,15 +413,19 @@
             side = jnp.where(lanes < 8, from_r, jnp.where(lanes >= 120, from_l, 0.0))
             side = jnp.where(gone, 0.0, side)
             if f < 6:
-                ref, c = fields[f]
+                ref, c = targets[f]
                 ref[c, nt, rows, :] = side
             else:
-                kh[rows, :] = side
-
-    unpack(rk[0], rk[1], own_r, False)
-    for i, rows in enumerate(keeps):
-        for f, (ref, c) in enumerate(fields):
-            keep[i, f, nt] = ref[c, nt, rows, :]
+                kh[lines, :] = side
+
+    unpack(rk[0], rk[1], fields, own_r, own_r, False)
+    rims = [
+        [(ref.at[side], c) for ref in (bu, bv, bs) for c in range(2)] for side in range(2)
+    ]
+    for side, (at, to) in enumerate(((8, 8), (frows - 16, 16))):
+        for (ref, c), (rim, _) in zip(fields, rims[side]):
+            for t in range(ntile):
+                rim[c, t, to : to + 8, :] = ref[c, t, at : at + 8, :]
 
     def edges(s):
         rows = slice(8 * s, 8 * s + 8)
@@ -449,21 +463,22 @@
                 su[c, t, rows, :] = su[c, t, rows, :] + v
 
     def interior(i, carry):
+        for f, (ref, c) in enumerate(fields):
+            at = frows - 24 + (f == 4)
+            for t in range(ntile):
+                past[i, 0, f, t] = ref[c, t, 16:24, :]
+                past[i, 1, f, t] = ref[c, t, at : at + 8, :]
         old = None
         for s in range(2, nstrip - 2):
-            if s == nstrip - 4:
-                for c in range(2):
-                    for t in range(ntile):
-                        hist_u[i, c, t] = su[c, t, 8 * s : 8 * s + 8, :]
             new = edges(s)
-            if s == 3:
-                for c in range(2):
-                    for t in range(ntile):
-                        hist_n[i, c, t] = nx[c, t, 8 * s : 8 * s + 8, :]
             if old:
                 advance(s - 1, old)
             old = new
         advance(nstrip - 3, old)
+        for c in range(2):
+            for t in range(ntile):
+                past_n[i, 0, c, t] = nx[c, t, 17:25, :]
+                past_n[i, 1, c, t] = nx[c, t, frows - 24 : frows - 16, :]
         return carry
 
     lax.fori_loop(0, SUBSTEPS, interior, 0)
@@ -499,42 +514,74 @@
     for s in (0, 1, 2, nstrip - 2, nstrip - 1):
         heat_x(s)
 
-    for side, (here, at) in enumerate(((has_u, 0), (has_d, hh + HALO))):
-        rows = slice(at, at + 8)
-        for f, (ref, c) in enumerate(fields):
+    for side, (here, at, to) in enumerate(((has_u, 0, 0), (has_d, hh + HALO, 24))):
+        rows = slice(to, to + 8)
+        lines = slice(at, at + 8)
+        for f, (rim, c) in enumerate(rims[side]):
             for t in range(nt):
-                ref[c, t, rows, :] = jnp.where(here, rowrecv[side, nt * f + t], 0.0)
-        kw[rows, :] = jnp.where(here, rowrecv[side, 6 * nt], 0.0)
-        unpack(ck[2 * side], ck[2 * side + 1], rows, ~here)
-    for i, rows in enumerate(keeps):
-        for f, (ref, c) in enumerate(fields):
-            for t in range(ntile):
-                ref[c, t, rows, :] = keep[i, f, t]
-    line = frows - 25
-    final = [[su[c, t, line : line + 1, :] for t in range(ntile)] for c in range(2)]
-    for c in range(2):
+                rim[c, t, rows, :] = jnp.where(here, rowrecv[side, nt * f + t], 0.0)
+        kw[lines, :] = jnp.where(here, rowrecv[side, 6 * nt], 0.0)
+        unpack(ck[2 * side], ck[2 * side + 1], rims[side], rows, lines, ~here)
+    for t in range(ntile):
+        bs[1, 0, t, 8:9, :] = ss[0, t, frows - 24 : frows - 23, :]
+
+    def rim_edges(side, x, y):
+        shift_by = (frows - 32) * side
+        u, spring, flow = bu.at[side], bs.at[side], bn.at[side]
+        ex, ex_up, ey = pl.ds(x, 8), pl.ds(x - 1, 8), pl.ds(y, 8)
+        gx_rows, gy_rows = pl.ds(x + shift_by, 8), pl.ds(y + shift_by, 8)
+        u0 = [u[0, t, ey, :] for t in range(ntile)]
+        u1 = [u[1, t, ey, :] for t in range(ntile)]
+        b0, b1 = before(u0), before(u1)
+        kx = [kw[gx_rows, :], kh[gx_rows, :]]
+        ky = [kw[gy_rows, :], kh[gy_rows, :]]
+        ay, ny = [], []
         for t in range(ntile):
-            hist_n[SUBSTEPS, c, t, 0:1, :] = final[c][t]
-
-    def border(i, carry):
+            open_x = u[0, t, ex, :] - u[0, t, ex_up, :] - tx[t, gx_rows, :]
+            st = jnp.maximum(open_x, 0.0)
+            sp = jnp.minimum(spring[0, t, ex, :], jnp.exp2(st * st * kx[t // nt]))
+            spring[0, t, ex, :] = sp
+            flow[0, t, ex, :] = sp * open_x
+            flow[1, t, ex, :] = sp * (u[1, t, ex, :] - u[1, t, ex_up, :])
+            open_y = u1[t] - b1[t] - ty[t, gy_rows, :]
+            st = jnp.maximum(open_y, 0.0)
+            sp = jnp.minimum(spring[1, t, ey, :], jnp.exp2(st * st * ky[t // nt]))
+            spring[1, t, ey, :] = sp
+            ny.append(sp * open_y)
+            ay.append(sp * (u0[t] - b0[t]))
+        fy0 = [a - b for a, b in zip(after(ay), ay)]
+        fy1 = [a - b for a, b in zip(after(ny), ny)]
+        return fy0, fy1
+
+    def rim_advance(side, y, fy):
+        rows, below = pl.ds(y, 8), pl.ds(y + 1, 8)
         for c in range(2):
             for t in range(ntile):
-                nx[c, t, 24:32, :] = hist_n[i, c, t]
-                su[c, t, line : line + 1, :] = hist_u[i, c, t, 7:8, :]
-        for at in (0, nstrip - 3):
-            old = None
-            for s in range(at, at + 3):
-                new = edges(s)
-                if old:
-                    advance(s - 1, old)
-                old = new
-            advance(at + 2, old)
-        return carry
-
-    lax.fori_loop(0, SUBSTEPS, border, 0)
-    for c in range(2):
+                force = (bn[side, c, t, below, :] - bn[side, c, t, rows, :]) + fy[c][t]
+                v = 0.98 * bv[side, c, t, rows, :] + 0.16 * force
+                bv[side, c, t, rows, :] = v
+                bu[side, c, t, rows, :] = bu[side, c, t, rows, :] + v
+
+    for i in range(SUBSTEPS):
         for t in range(ntile):
-            su[c, t, line : line + 1, :] = hist_n[SUBSTEPS, c, t, 0:1, :]
+            for f in range(6):
+                rim, c = rims[0][f]
+                rim[c, t, 16 + i : 17 + i, :] = past[i, 0, f, t, i : i + 1, :]
+                rim, c = rims[1][f]
+                to = 15 - i + (f == 4)
+                rim[c, t, to : to + 1, :] = past[i, 1, f, t, 7 - i : 8 - i, :]
+            for c in range(2):
+                bn[0, c, t, 17 + i : 18 + i, :] = past_n[i, 0, c, t, i : i + 1, :]
+                bn[1, c, t, 15 - i : 16 - i, :] = past_n[i, 1, c, t, 7 - i : 8 - i, :]
+        for side, x, y in ((0, i + 1, i + 1), (1, 16 - i, 15 - i)):
+            first = rim_edges(side, x, y)
+            second = rim_edges(side, x + 8, y + 8)
+            rim_advance(side, y, first)
+            rim_advance(side, y + 8, second)
+    for side, at in ((0, 8), (1, frows - 24)):
+        for (ref, c), (rim, _) in zip(fields, rims[side]):
+            for t in range(nt):
+                ref[c, t, at : at + 16, :] = rim[c, t, 8:24, :]
 
     for t in range(nt):
         gcol = gy * ww + 128 * t + lane
@@ -649,8 +696,8 @@
             peak = ratio if peak is None else jnp.maximum(peak, ratio)
     msend[...] = jnp.full((1, 128), jnp.max(peak), F32)
 
-    for k in range(1, ndev):
-        t = lax.rem(me + k, ndev)
+    for k in far_first(ndev, lambda k: k % n_gy // 2 + (k // n_gy).bit_count()):
+        t = partner(me, k, ndev)
         remote(
             msend, mrecv.at[k - 1], s_sem.at[0], r_sem.at[8], (t // n_gy, t % n_gy)
         ).start()
@@ -811,9 +858,12 @@
             vm(4, 8, 128),
             vm(2, 6 * nt + 1, 8, 128),
             vm(2, 6 * nt + 1, 8, 128),
-            vm(2, 6, ntile, 8, 128),
-            vm(SUBSTEPS + 1, 2, ntile, 8, 128),
-            vm(SUBSTEPS, 2, ntile, 8, 128),
+            vm(2, 2, ntile, 32, 128),
+            vm(2, 2, ntile, 32, 128),
+            vm(2, 2, ntile, 32, 128),
+            vm(2, 2, ntile, 40, 128),
+            vm(SUBSTEPS, 2, 6, ntile, 8, 128),
+            vm(SUBSTEPS, 2, 2, ntile, 8, 128),
             pltpu.VMEM(level.shape, level.dtype),
             vm(*warm.shape),
             vm(*warm.shape),

time: 25.1 us -> 24.5 us (0.976)
  Pallas kernels: 24.3 us -> 23.7 us
    pallas_call x1, Pallas kernels: 23.4 us -> 22.9 us  [per_device(): pl.pallas_call(functools.partial(kernel, n_gx, n_gy), out_shape=(vm(2, nt...]
where the time goes in v4:
time: 24.5 us; the launch traced here: 24.4 us
  Pallas kernels  23.7 us (97%)
  between operations  0.64 us (3%)
    pallas_call x1, Pallas kernels, per_device(): pl.pallas_call(functools.partial(kernel, n_gx, n_gy), out_shape=(vm(2, nt...  22.9 us
    pallas_call x1, Pallas kernels, per_device(): pl.pallas_call(put_out, out_shape=tuple((jax.ShapeDtypeStruct(o.shape, d)...  0.87 us

profile of v4, /device:TPU:0, one launch (start us, length us, event | category | flops | bytes accessed | tf_op | source)
XLA Modules:
  0.0 24.4 jit_solution(5710883695055341876)
XLA Ops:
  0.6 22.9 %shard_map.111 = (f32[2,5,80,128]{3,2,1,0:T(8,128)S(1)}, f32[2,4,64,128]{3,2,1,0:T(8,128)S(1)}, bf16[2,4,64,128]{3,2,1,0:T(8,128)(2,1)S(1)}, f32[4,2048]{1,0:T(4,128)S(1)}) custom-call(f32[2,64,512]{2,1,0:T(8,128)} %shift.1, f32[2,64,512]{2,1,0:T(8,128)} %speed.1, s32[2,64,512]{2,1,0:T(8,128)} %level_h.1, s32[1,8]{1,0:T(1,128)} %bitcast.1, ...), custom_call_target="tpu_custom_call" | custom-call | tf_op jit(solution)/shard_map/pallas_call | solution.py:841
  23.5 0.9 %shard_map.112 = (f32[2,64,512]{2,1,0:T(8,128)}, f32[2,64,512]{2,1,0:T(8,128)}, bf16[2,64,512]{2,1,0:T(8,128)(2,1)}, f32[4,2048]{1,0:T(4,128)}) custom-call(f32[2,5,80,128]{3,2,1,0:T(8,128)S(1)} %get-tuple-element.8.su, f32[2,4,64,128]{3,2,1,0:T(8,128)S(1)} %get-tuple-element.9.speed, bf16[2,4,64,128]{3,2,1,0:T(8,128)(2,1)S(1)} %get-tuple-element.10.dam, ...), custom_call_target="tpu_custom_call" | custom-call | tf_op jit(solution)/shard_map/pallas_call | solution.py:906

commit v5 on v4

--- a/solution.py
+++ b/solution.py
@@ -163,11 +163,17 @@
 
     for k in far_first(n_gy, lambda k: k // 2):
         greet(gx, partner(gy, k, n_gy))
+    calls = n_gy - 1
     for k in range(1, n_gx):
-        greet(lax.rem(gx + k, n_gx), gy)
-    for a in (up, down):
-        for b in (left, right):
-            greet(a, b)
+        if k == 1 or k > 3:
+            for ok, a in ((gx >= k, gx - k), (gx + k < n_gx, gx + k)):
+                sides = ((True, gy), (has_l, left), (has_r, right)) if k == 1 else ((True, gy),)
+                for beside, b in sides:
+                    calls = calls + jnp.where(ok & beside, 1, 0)
+
+                    @pl.when(ok & beside)
+                    def _():
+                        greet(a, b)
 
     loads = [
         pltpu.make_async_copy(src, dst, r_sem.at[i])
@@ -209,13 +215,6 @@
         tsend[k, :, 0:cw] = main
         tsend[k, :, cw : cw + 128] = edge
 
-    pl.semaphore_wait(barrier, n_gy + n_gx + 2)
-
-    for k in far_first(n_gy, lambda k: k // 2):
-        t = partner(gy, k, n_gy)
-        remote(tsend.at[t], trecv.at[gy + hb], s_sem.at[0], r_sem.at[3], (gx, t)).start()
-    pltpu.make_async_copy(tsend.at[gy], trecv.at[gy + hb], r_sem.at[3]).start()
-
     sharp = -4.0 * math.log2(math.e)
     lane = lane_iota((hh, 128))
     loads[0].wait()
@@ -234,6 +233,8 @@
     for c in range(2):
         for t in range(nt):
             sv[c, t, own_r, :] = 0.4 * sv[c, t, own_r, :]
+    lines_of = (8, 8, 7, 7, 8, 7)
+    line_at = [nt * sum(lines_of[:f]) for f in range(7)]
     acc_l = jnp.zeros((hh, 128), F32)
     acc_r = jnp.zeros((hh, 128), F32)
     fields = [(ref, c) for ref in (su, sv, ss) for c in range(2)]
@@ -273,14 +274,25 @@
         def _():
             copy.wait_send()
 
-    for cond, copy in sends[0:6]:
-        start_if(cond, copy)
     for side, at in ((0, HALO), (1, HALO + hh - 8)):
         for f, (ref, c) in enumerate(fields):
+            skip = side if lines_of[f] == 7 else 0
             for t in range(nt):
-                rowsend[side, nt * f + t] = ref[c, t, at : at + 8, :]
-        rowsend[side, 6 * nt] = kw[at : at + 8, :]
+                to = line_at[f] + lines_of[f] * t
+                rowsend[side, to : to + lines_of[f], :] = ref[
+                    c, t, at + skip : at + skip + lines_of[f], :
+                ]
+        rowsend[side, line_at[6] : line_at[6] + 1, :] = kw[at : at + 1, :]
+    pl.semaphore_wait(barrier, calls)
+
+    for k in far_first(n_gy, lambda k: k // 2):
+        t = partner(gy, k, n_gy)
+        remote(tsend.at[t], trecv.at[gy + hb], s_sem.at[0], r_sem.at[3], (gx, t)).start()
+    pltpu.make_async_copy(tsend.at[gy], trecv.at[gy + hb], r_sem.at[3]).start()
+
     for cond, copy in sends[6:8]:
+        start_if(cond, copy)
+    for cond, copy in sends[0:6]:
         start_if(cond, copy)
 
     k_i, n_i = row_iota((256, 128)), lane_iota((256, 128))
@@ -302,10 +314,10 @@
     mid = trecv.at[pl.ds(hb, n_gy)]
     pltpu.make_async_copy(mid, mid, r_sem.at[3]).wait()
     far_u = remote(
-        trecv.at[pl.ds(hb, hb)], trecv.at[pl.ds(hb + n_gy, hb)], s_sem.at[1], r_sem.at[2], (up, gy)
+        trecv.at[pl.ds(hb, hb)], trecv.at[pl.ds(hb + n_gy, hb)], s_sem.at[1], r_sem.at[12], (up, gy)
     )
     far_d = remote(
-        trecv.at[pl.ds(n_gy, hb)], trecv.at[pl.ds(0, hb)], s_sem.at[2], r_sem.at[2], (down, gy)
+        trecv.at[pl.ds(n_gy, hb)], trecv.at[pl.ds(0, hb)], s_sem.at[2], r_sem.at[12], (down, gy)
     )
     start_if(has_u, far_u)
     start_if(has_d, far_d)
@@ -489,8 +501,22 @@
             done_if(
                 (n_v == v) & (n_h == h),
                 r_sem.at[2],
-                v * (size(rowsend.at[0]) + far_size + h * size(ck.at[0])),
+                v * (size(rowsend.at[0]) + h * size(ck.at[0])),
             )
+    for side, (here, at, to) in enumerate(((has_u, 0, 0), (has_d, hh + HALO, 24))):
+        rows = slice(to, to + 8)
+        lines = slice(at, at + 8)
+        for f, (rim, c) in enumerate(rims[side]):
+            first = to if side or lines_of[f] == 8 else to + 1
+            for t in range(nt):
+                line = line_at[f] + lines_of[f] * t
+                got = rowrecv[side, line : line + lines_of[f], :]
+                rim[c, t, first : first + lines_of[f], :] = jnp.where(here, got, 0.0)
+        got = jnp.broadcast_to(rowrecv[side, line_at[6] : line_at[6] + 1, :], (8, 128))
+        kw[lines, :] = jnp.where(here, got, 0.0)
+        unpack(ck[2 * side], ck[2 * side + 1], rims[side], rows, lines, ~here)
+    for v in (1, 2):
+        done_if(n_v == v, r_sem.at[12], v * far_size)
     for side, (here, at, slot, line) in enumerate(
         ((has_u, 0, 0, 8), (has_d, ch + 8, hb + n_gy, ch + 7))
     ):
@@ -514,14 +540,6 @@
     for s in (0, 1, 2, nstrip - 2, nstrip - 1):
         heat_x(s)
 
-    for side, (here, at, to) in enumerate(((has_u, 0, 0), (has_d, hh + HALO, 24))):
-        rows = slice(to, to + 8)
-        lines = slice(at, at + 8)
-        for f, (rim, c) in enumerate(rims[side]):
-            for t in range(nt):
-                rim[c, t, rows, :] = jnp.where(here, rowrecv[side, nt * f + t], 0.0)
-        kw[lines, :] = jnp.where(here, rowrecv[side, 6 * nt], 0.0)
-        unpack(ck[2 * side], ck[2 * side + 1], rims[side], rows, lines, ~here)
     for t in range(ntile):
         bs[1, 0, t, 8:9, :] = ss[0, t, frows - 24 : frows - 23, :]
 
@@ -856,8 +874,8 @@
             vm(2, hh, 128),
             vm(2, hh, 128),
             vm(4, 8, 128),
-            vm(2, 6 * nt + 1, 8, 128),
-            vm(2, 6 * nt + 1, 8, 128),
+            vm(2, 45 * nt + 1, 128),
+            vm(2, 45 * nt + 1, 128),
             vm(2, 2, ntile, 32, 128),
             vm(2, 2, ntile, 32, 128),
             vm(2, 2, ntile, 32, 128),
@@ -895,7 +913,7 @@
             vm(1, 128),
             vm(n_gx * n_gy - 1, 1, 128),
             dma(5 + 2 * hz),
-            dma(12),
+            dma(13),
             vm(3 * level.size // 128, 1, 128),
             pltpu.SMEM((1, hh // SR), mark.dtype),
         ],

time: 24.5 us -> 24 us (0.980)
  Pallas kernels: 23.7 us -> 23.2 us
    pallas_call x1, Pallas kernels: 22.9 us -> 22.4 us  [per_device(): pl.pallas_call(functools.partial(kernel, n_gx, n_gy), out_shape=(vm(2, nt...]
where the time goes in v5:
time: 24 us; the launch traced here: 23.9 us
  Pallas kernels  23.2 us (97%)
  between operations  0.64 us (3%)
    pallas_call x1, Pallas kernels, per_device(): pl.pallas_call(functools.partial(kernel, n_gx, n_gy), out_shape=(vm(2, nt...  22.4 us
    pallas_call x1, Pallas kernels, per_device(): pl.pallas_call(put_out, out_shape=tuple((jax.ShapeDtypeStruct(o.shape, d)...  0.87 us

profile of v5, /device:TPU:0, one launch (start us, length us, event | category | flops | bytes accessed | tf_op | source)
XLA Modules:
  0.0 23.9 jit_solution(15730925141148719174)
XLA Ops:
  0.6 22.4 %shard_map.111 = (f32[2,5,80,128]{3,2,1,0:T(8,128)S(1)}, f32[2,4,64,128]{3,2,1,0:T(8,128)S(1)}, bf16[2,4,64,128]{3,2,1,0:T(8,128)(2,1)S(1)}, f32[4,2048]{1,0:T(4,128)S(1)}) custom-call(f32[2,64,512]{2,1,0:T(8,128)} %shift.1, f32[2,64,512]{2,1,0:T(8,128)} %speed.1, s32[2,64,512]{2,1,0:T(8,128)} %level_h.1, s32[1,8]{1,0:T(1,128)} %bitcast.1, ...), custom_call_target="tpu_custom_call" | custom-call | tf_op jit(solution)/shard_map/pallas_call | solution.py:859
  23.0 0.9 %shard_map.112 = (f32[2,64,512]{2,1,0:T(8,128)}, f32[2,64,512]{2,1,0:T(8,128)}, bf16[2,64,512]{2,1,0:T(8,128)(2,1)}, f32[4,2048]{1,0:T(4,128)}) custom-call(f32[2,5,80,128]{3,2,1,0:T(8,128)S(1)} %get-tuple-element.8.su, f32[2,4,64,128]{3,2,1,0:T(8,128)S(1)} %get-tuple-element.9.speed, bf16[2,4,64,128]{3,2,1,0:T(8,128)(2,1)S(1)} %get-tuple-element.10.dam, ...), custom_call_target="tpu_custom_call" | custom-call | tf_op jit(solution)/shard_map/pallas_call | solution.py:924

commit v6 on v5

--- a/solution.py
+++ b/solution.py
@@ -26,7 +26,7 @@
 
 
 def full_dot(a, b):
-    return jnp.dot(a, b, precision=lax.Precision.HIGHEST, preferred_element_type=F32)
+    return jnp.dot(a, b, precision=lax.Precision.HIGH, preferred_element_type=F32)
 
 
 def partner(me, k, n):
@@ -77,6 +77,7 @@
     bn,
     past,
     past_n,
+    way,
     level,
     warm,
     store,
@@ -164,6 +165,14 @@
     for k in far_first(n_gy, lambda k: k // 2):
         greet(gx, partner(gy, k, n_gy))
     calls = n_gy - 1
+    detour = n_gx == 4
+    if detour:
+        calls = calls + jnp.where((gx == 1) | (gx == 2), 1, 0)
+
+        @pl.when((gx == 0) | (gx == 3))
+        def _():
+            greet(lax.rem(gx + 2, n_gx), gy)
+
     for k in range(1, n_gx):
         if k == 1 or k > 3:
             for ok, a in ((gx >= k, gx - k), (gx + k < n_gx, gx + k)):
@@ -259,10 +268,30 @@
         (has_d & has_l, remote(pk.at[0, end], ck.at[1], s_sem.at[2], r_sem.at[2], (down, left)), 4),
         (has_d & has_r, remote(pk.at[1, end], ck.at[0], s_sem.at[2], r_sem.at[2], (down, right)), 5),
     ]
-    rows_u = remote(rowsend.at[0], rowrecv.at[1], s_sem.at[1], r_sem.at[2], (up, gy))
-    rows_d = remote(rowsend.at[1], rowrecv.at[0], s_sem.at[2], r_sem.at[2], (down, gy))
+    n_lines = rowsend.shape[1]
+    turn = 96 if n_gx == 4 else n_lines
+    head, rest = pl.ds(0, turn), pl.ds(turn, n_lines - turn)
+    row_sends = [
+        (has_u, remote(rowsend.at[0, head], rowrecv.at[1, head], s_sem.at[1], r_sem.at[2], (up, gy))),
+        (has_d, remote(rowsend.at[1, head], rowrecv.at[0, head], s_sem.at[2], r_sem.at[2], (down, gy))),
+    ]
+    if detour:
+        across = lax.rem(gx + 2, n_gx)
+        for straight, around, side, sem, to in (
+            (has_u & (gx != 2), gx == 2, 0, 1, up),
+            (has_d & (gx != 1), gx == 1, 1, 2, down),
+        ):
+            src = rowsend.at[side, rest]
+            row_sends += [
+                (around, remote(src, way, s_sem.at[sem], r_sem.at[13], (across, gy))),
+                (straight, remote(src, rowrecv.at[1 - side, rest], s_sem.at[sem], r_sem.at[2], (to, gy))),
+            ]
+        pass_on = [
+            (gx == 0, remote(way, rowrecv.at[1, rest], s_sem.at[5 + 2 * hz], r_sem.at[2], (down, gy))),
+            (gx == 3, remote(way, rowrecv.at[0, rest], s_sem.at[5 + 2 * hz], r_sem.at[2], (up, gy))),
+        ]
     sends = [(has_l, side_l), (has_r, side_r)] + [(a, b) for a, b, _ in corners]
-    sends += [(has_u, rows_u), (has_d, rows_d)]
+    sends += row_sends
 
     def start_if(cond, copy):
         @pl.when(cond)
@@ -290,7 +319,7 @@
         remote(tsend.at[t], trecv.at[gy + hb], s_sem.at[0], r_sem.at[3], (gx, t)).start()
     pltpu.make_async_copy(tsend.at[gy], trecv.at[gy + hb], r_sem.at[3]).start()
 
-    for cond, copy in sends[6:8]:
+    for cond, copy in sends[6:]:
         start_if(cond, copy)
     for cond, copy in sends[0:6]:
         start_if(cond, copy)
@@ -311,6 +340,37 @@
     nx[:, :, strip : strip + 8, :] = jnp.zeros((2, ntile, 8, 128), F32)
     bn[:, :, :, 32:40, :] = jnp.zeros((2, 2, ntile, 8, 128), F32)
 
+    for h in (1, 2):
+        done_if(n_h == h, r_sem.at[0], h * size(pk.at[0]))
+
+    def unpack(got_l, got_r, targets, rows, lines, outside):
+        shape = got_l.shape
+        lanes = lane_iota(shape)
+        gone = outside | (~has_l & (lanes >= 64)) | (~has_r & (lanes < 64))
+        for f in range(FIELDS):
+            from_r = pltpu.roll(got_r, 128 - 8 * f, 1) if f else got_r
+            from_l = pltpu.roll(got_l, 120 - 8 * f, 1)
+            side = jnp.where(lanes < 8, from_r, jnp.where(lanes >= 120, from_l, 0.0))
+            side = jnp.where(gone, 0.0, side)
+            if f < 6:
+                ref, c = targets[f]
+                ref[c, nt, rows, :] = side
+            else:
+                kh[lines, :] = side
+
+    unpack(rk[0], rk[1], fields, own_r, own_r, False)
+    rims = [
+        [(ref.at[side], c) for ref in (bu, bv, bs) for c in range(2)] for side in range(2)
+    ]
+    for side, (at, to) in enumerate(((8, 8), (frows - 16, 16))):
+        for (ref, c), (rim, _) in zip(fields, rims[side]):
+            for t in range(ntile):
+                rim[c, t, to : to + 8, :] = ref[c, t, at : at + 8, :]
+
+    if detour:
+        done_if((gx == 0) | (gx == 3), r_sem.at[13], size(way))
+        for cond, copy in pass_on:
+            start_if(cond, copy)
     mid = trecv.at[pl.ds(hb, n_gy)]
     pltpu.make_async_copy(mid, mid, r_sem.at[3]).wait()
     far_u = remote(
@@ -412,33 +472,6 @@
     for s in range(2, nstrip - 2):
         heat_x(s)
 
-    for h in (1, 2):
-        done_if(n_h == h, r_sem.at[0], h * size(pk.at[0]))
-
-    def unpack(got_l, got_r, targets, rows, lines, outside):
-        shape = got_l.shape
-        lanes = lane_iota(shape)
-        gone = outside | (~has_l & (lanes >= 64)) | (~has_r & (lanes < 64))
-        for f in range(FIELDS):
-            from_r = pltpu.roll(got_r, 128 - 8 * f, 1) if f else got_r
-            from_l = pltpu.roll(got_l, 120 - 8 * f, 1)
-            side = jnp.where(lanes < 8, from_r, jnp.where(lanes >= 120, from_l, 0.0))
-            side = jnp.where(gone, 0.0, side)
-            if f < 6:
-                ref, c = targets[f]
-                ref[c, nt, rows, :] = side
-            else:
-                kh[lines, :] = side
-
-    unpack(rk[0], rk[1], fields, own_r, own_r, False)
-    rims = [
-        [(ref.at[side], c) for ref in (bu, bv, bs) for c in range(2)] for side in range(2)
-    ]
-    for side, (at, to) in enumerate(((8, 8), (frows - 16, 16))):
-        for (ref, c), (rim, _) in zip(fields, rims[side]):
-            for t in range(ntile):
-                rim[c, t, to : to + 8, :] = ref[c, t, at : at + 8, :]
-
     def edges(s):
         rows = slice(8 * s, 8 * s + 8)
         u0 = [su[0, t, rows, :] for t in range(ntile)]
@@ -596,18 +629,18 @@
             second = rim_edges(side, x + 8, y + 8)
             rim_advance(side, y, first)
             rim_advance(side, y + 8, second)
-    for side, at in ((0, 8), (1, frows - 24)):
-        for (ref, c), (rim, _) in zip(fields, rims[side]):
-            for t in range(nt):
-                ref[c, t, at : at + 16, :] = rim[c, t, 8:24, :]
-
+    def settle(some):
+        for side, at in ((0, 8), (1, frows - 24)):
+            for (ref, c), (rim, _) in zip(some(fields), some(rims[side])):
+                for t in range(nt):
+                    ref[c, t, at : at + 16, :] = rim[c, t, 8:24, :]
+
+    settle(lambda x: x[4:6])
     for t in range(nt):
         gcol = gy * ww + 128 * t + lane
         dam_x = jnp.where(grow >= 1, 1.0 - ss[0, t, own_r, :], 0.0)
         dam_y = jnp.where(gcol >= 1, 1.0 - ss[1, t, own_r, :], 0.0)
         gap[t] = dam_x + dam_y
-        o_dam[0, t] = dam_x.astype(jnp.bfloat16)
-        o_dam[1, t] = dam_y.astype(jnp.bfloat16)
     rows2 = jnp.concatenate(
         [
             gap[t, pl.ds(0, ch, stride=2), :] + gap[t, pl.ds(1, ch, stride=2), :]
@@ -666,9 +699,16 @@
     for ok, copy in to_owner:
         start_if(ok, copy)
 
+    settle(lambda x: x[0:4])
     for c in range(2):
         for t in range(nt):
             o_speed[c, t] = 2.5 * sv[c, t, own_r, :]
+    for t in range(nt):
+        gcol = gy * ww + 128 * t + lane
+        dam_x = jnp.where(grow >= 1, 1.0 - ss[0, t, own_r, :], 0.0)
+        dam_y = jnp.where(gcol >= 1, 1.0 - ss[1, t, own_r, :], 0.0)
+        o_dam[0, t] = dam_x.astype(jnp.bfloat16)
+        o_dam[1, t] = dam_y.astype(jnp.bfloat16)
 
     pltpu.make_async_copy(arecv, arecv, r_sem.at[4]).wait()
     for k in range(n_gy):
@@ -819,6 +859,8 @@
     for i, ok in ((1, has_u), (2, has_d)):
         for h in (1, 2):
             done_if(ok & (n_h == h), s_sem.at[i], tall + h * size(ck.at[0]))
+    if detour:
+        done_if((gx == 0) | (gx == 3), s_sem.at[5 + 2 * hz], size(way))
     for i, ok in ((3, has_l), (4, has_r)):
         done_if(ok, s_sem.at[i], size(pk.at[0]) + size(ecol.at[0]))
 
@@ -882,6 +924,7 @@
             vm(2, 2, ntile, 40, 128),
             vm(SUBSTEPS, 2, 6, ntile, 8, 128),
             vm(SUBSTEPS, 2, 2, ntile, 8, 128),
+            vm(45 * nt + 1 - 96, 128),
             pltpu.VMEM(level.shape, level.dtype),
             vm(*warm.shape),
             vm(*warm.shape),
@@ -912,8 +955,8 @@
             vm(4, rpd, cw * n_gy),
             vm(1, 128),
             vm(n_gx * n_gy - 1, 1, 128),
-            dma(5 + 2 * hz),
-            dma(13),
+            dma(6 + 2 * hz),
+            dma(14),
             vm(3 * level.size // 128, 1, 128),
             pltpu.SMEM((1, hh // SR), mark.dtype),
         ],

time: 24 us -> 24 us (level)
  no operation moved by 1% of the time
where the time goes in v6:
time: 24 us; the launch traced here: 23.9 us
  Pallas kernels  23.2 us (97%)
  between operations  0.64 us (3%)
    pallas_call x1, Pallas kernels, per_device(): pl.pallas_call(functools.partial(kernel, n_gx, n_gy), out_shape=(vm(2, nt...  22.4 us
    pallas_call x1, Pallas kernels, per_device(): pl.pallas_call(put_out, out_shape=tuple((jax.ShapeDtypeStruct(o.shape, d)...  0.87 us

profile of v6, /device:TPU:0, one launch (start us, length us, event | category | flops | bytes accessed | tf_op | source)
XLA Modules:
  0.0 23.9 jit_solution(8468004591677825759)
XLA Ops:
  0.6 22.4 %shard_map.111 = (f32[2,5,80,128]{3,2,1,0:T(8,128)S(1)}, f32[2,4,64,128]{3,2,1,0:T(8,128)S(1)}, bf16[2,4,64,128]{3,2,1,0:T(8,128)(2,1)S(1)}, f32[4,2048]{1,0:T(4,128)S(1)}) custom-call(f32[2,64,512]{2,1,0:T(8,128)} %shift.1, f32[2,64,512]{2,1,0:T(8,128)} %speed.1, s32[2,64,512]{2,1,0:T(8,128)} %level_h.1, s32[1,8]{1,0:T(1,128)} %bitcast.1, ...), custom_call_target="tpu_custom_call" | custom-call | tf_op jit(solution)/shard_map/pallas_call | solution.py:901
  23.0 0.9 %shard_map.112 = (f32[2,64,512]{2,1,0:T(8,128)}, f32[2,64,512]{2,1,0:T(8,128)}, bf16[2,64,512]{2,1,0:T(8,128)(2,1)}, f32[4,2048]{1,0:T(4,128)}) custom-call(f32[2,5,80,128]{3,2,1,0:T(8,128)S(1)} %get-tuple-element.8.su, f32[2,4,64,128]{3,2,1,0:T(8,128)S(1)} %get-tuple-element.9.speed, bf16[2,4,64,128]{3,2,1,0:T(8,128)(2,1)S(1)} %get-tuple-element.10.dam, ...), custom_call_target="tpu_custom_call" | custom-call | tf_op jit(solution)/shard_map/pallas_call | solution.py:967

commit v7 on v6

--- a/solution.py
+++ b/solution.py
@@ -77,7 +77,6 @@
     bn,
     past,
     past_n,
-    way,
     level,
     warm,
     store,
@@ -165,14 +164,6 @@
     for k in far_first(n_gy, lambda k: k // 2):
         greet(gx, partner(gy, k, n_gy))
     calls = n_gy - 1
-    detour = n_gx == 4
-    if detour:
-        calls = calls + jnp.where((gx == 1) | (gx == 2), 1, 0)
-
-        @pl.when((gx == 0) | (gx == 3))
-        def _():
-            greet(lax.rem(gx + 2, n_gx), gy)
-
     for k in range(1, n_gx):
         if k == 1 or k > 3:
             for ok, a in ((gx >= k, gx - k), (gx + k < n_gx, gx + k)):
@@ -268,30 +259,10 @@
         (has_d & has_l, remote(pk.at[0, end], ck.at[1], s_sem.at[2], r_sem.at[2], (down, left)), 4),
         (has_d & has_r, remote(pk.at[1, end], ck.at[0], s_sem.at[2], r_sem.at[2], (down, right)), 5),
     ]
-    n_lines = rowsend.shape[1]
-    turn = 96 if n_gx == 4 else n_lines
-    head, rest = pl.ds(0, turn), pl.ds(turn, n_lines - turn)
-    row_sends = [
-        (has_u, remote(rowsend.at[0, head], rowrecv.at[1, head], s_sem.at[1], r_sem.at[2], (up, gy))),
-        (has_d, remote(rowsend.at[1, head], rowrecv.at[0, head], s_sem.at[2], r_sem.at[2], (down, gy))),
-    ]
-    if detour:
-        across = lax.rem(gx + 2, n_gx)
-        for straight, around, side, sem, to in (
-            (has_u & (gx != 2), gx == 2, 0, 1, up),
-            (has_d & (gx != 1), gx == 1, 1, 2, down),
-        ):
-            src = rowsend.at[side, rest]
-            row_sends += [
-                (around, remote(src, way, s_sem.at[sem], r_sem.at[13], (across, gy))),
-                (straight, remote(src, rowrecv.at[1 - side, rest], s_sem.at[sem], r_sem.at[2], (to, gy))),
-            ]
-        pass_on = [
-            (gx == 0, remote(way, rowrecv.at[1, rest], s_sem.at[5 + 2 * hz], r_sem.at[2], (down, gy))),
-            (gx == 3, remote(way, rowrecv.at[0, rest], s_sem.at[5 + 2 * hz], r_sem.at[2], (up, gy))),
-        ]
+    rows_u = remote(rowsend.at[0], rowrecv.at[1], s_sem.at[1], r_sem.at[2], (up, gy))
+    rows_d = remote(rowsend.at[1], rowrecv.at[0], s_sem.at[2], r_sem.at[2], (down, gy))
     sends = [(has_l, side_l), (has_r, side_r)] + [(a, b) for a, b, _ in corners]
-    sends += row_sends
+    sends += [(has_u, rows_u), (has_d, rows_d)]
 
     def start_if(cond, copy):
         @pl.when(cond)
@@ -319,7 +290,7 @@
         remote(tsend.at[t], trecv.at[gy + hb], s_sem.at[0], r_sem.at[3], (gx, t)).start()
     pltpu.make_async_copy(tsend.at[gy], trecv.at[gy + hb], r_sem.at[3]).start()
 
-    for cond, copy in sends[6:]:
+    for cond, copy in sends[6:8]:
         start_if(cond, copy)
     for cond, copy in sends[0:6]:
         start_if(cond, copy)
@@ -367,10 +338,6 @@
             for t in range(ntile):
                 rim[c, t, to : to + 8, :] = ref[c, t, at : at + 8, :]
 
-    if detour:
-        done_if((gx == 0) | (gx == 3), r_sem.at[13], size(way))
-        for cond, copy in pass_on:
-            start_if(cond, copy)
     mid = trecv.at[pl.ds(hb, n_gy)]
     pltpu.make_async_copy(mid, mid, r_sem.at[3]).wait()
     far_u = remote(
@@ -859,8 +826,6 @@
     for i, ok in ((1, has_u), (2, has_d)):
         for h in (1, 2):
             done_if(ok & (n_h == h), s_sem.at[i], tall + h * size(ck.at[0]))
-    if detour:
-        done_if((gx == 0) | (gx == 3), s_sem.at[5 + 2 * hz], size(way))
     for i, ok in ((3, has_l), (4, has_r)):
         done_if(ok, s_sem.at[i], size(pk.at[0]) + size(ecol.at[0]))
 
@@ -924,7 +889,6 @@
             vm(2, 2, ntile, 40, 128),
             vm(SUBSTEPS, 2, 6, ntile, 8, 128),
             vm(SUBSTEPS, 2, 2, ntile, 8, 128),
-            vm(45 * nt + 1 - 96, 128),
             pltpu.VMEM(level.shape, level.dtype),
             vm(*warm.shape),
             vm(*warm.shape),
@@ -955,8 +919,8 @@
             vm(4, rpd, cw * n_gy),
             vm(1, 128),
             vm(n_gx * n_gy - 1, 1, 128),
-            dma(6 + 2 * hz),
-            dma(14),
+            dma(5 + 2 * hz),
+            dma(13),
             vm(3 * level.size // 128, 1, 128),
             pltpu.SMEM((1, hh // SR), mark.dtype),
         ],

time: 24 us -> 24 us (level)
  no operation moved by 1% of the time
where the time goes in v7:
time: 24 us; the launch traced here: 23.8 us
  Pallas kernels  23.2 us (97%)
  between operations  0.64 us (3%)
    pallas_call x1, Pallas kernels, per_device(): pl.pallas_call(functools.partial(kernel, n_gx, n_gy), out_shape=(vm(2, nt...  22.3 us
    pallas_call x1, Pallas kernels, per_device(): pl.pallas_call(put_out, out_shape=tuple((jax.ShapeDtypeStruct(o.shape, d)...  0.87 us

profile of v7, /device:TPU:0, one launch (start us, length us, event | category | flops | bytes accessed | tf_op | source)
XLA Modules:
  0.0 23.8 jit_solution(10147237147500642573)
XLA Ops:
  0.6 22.3 %shard_map.111 = (f32[2,5,80,128]{3,2,1,0:T(8,128)S(1)}, f32[2,4,64,128]{3,2,1,0:T(8,128)S(1)}, bf16[2,4,64,128]{3,2,1,0:T(8,128)(2,1)S(1)}, f32[4,2048]{1,0:T(4,128)S(1)}) custom-call(f32[2,64,512]{2,1,0:T(8,128)} %shift.1, f32[2,64,512]{2,1,0:T(8,128)} %speed.1, s32[2,64,512]{2,1,0:T(8,128)} %level_h.1, s32[1,8]{1,0:T(1,128)} %bitcast.1, ...), custom_call_target="tpu_custom_call" | custom-call | tf_op jit(solution)/shard_map/pallas_call | solution.py:866
  22.9 0.9 %shard_map.112 = (f32[2,64,512]{2,1,0:T(8,128)}, f32[2,64,512]{2,1,0:T(8,128)}, bf16[2,64,512]{2,1,0:T(8,128)(2,1)}, f32[4,2048]{1,0:T(4,128)}) custom-call(f32[2,5,80,128]{3,2,1,0:T(8,128)S(1)} %get-tuple-element.8.su, f32[2,4,64,128]{3,2,1,0:T(8,128)S(1)} %get-tuple-element.9.speed, bf16[2,4,64,128]{3,2,1,0:T(8,128)(2,1)S(1)} %get-tuple-element.10.dam, ...), custom_call_target="tpu_custom_call" | custom-call | tf_op jit(solution)/shard_map/pallas_call | solution.py:931
